TPU v7x, 256 devices: a whole 4x4x8 slice. The times are simulated.
256 devices in a mesh: phase: 8 (over z_lo, x), ctx: 32 (over y, z_hi, core).
Axes of the slice: x: 4, y: 4, z: 8 (z_hi: 4, z_lo: 2; z = z_hi * 2 + z_lo), core: 2. Of those that a mesh axis runs over, the one named last changes fastest.
Arguments:
- inputs: bfloat16 [1, 4096, 2048], P(None, 'ctx'), may hold values from -6 to 6
- segment_ids: int32 [1, 4096], P(None, 'ctx'), may hold values from 0 to 15, never falling along the last dimension, each value on 1 to 768 neighbouring positions
- w_query: bfloat16 [8, 2048, 1024], P('phase'), may hold values from -1 to 1
- w_keyval: bfloat16 [8, 2048, 2048], P('phase', 'ctx'), may hold values from -16 to 16
- w_out: bfloat16 [8, 1024, 2048], P('phase'), may hold values from -0.1875 to 0.1875
Outputs:
- section_out: bfloat16 [8, 1, 4096, 2048], P('phase', None, 'ctx')
Inputs may be any that keep to these rules, and one draw needn't show every extreme that they name: `segment_ids`: ids never fall along the tokens of a micro-batch; each trajectory is a run of 1 to 768 tokens and one run has exactly 768.
All inputs are finite; a program needn't handle non-finite values.
Results may differ from a plain program's by a relative error of at most 0.015.
Values may be sent and summed in bfloat16 or wider, within the bound.
A program may use at most 64 MiB of HBM per device.

v0:
```python
import math

import jax
import jax.numpy as jnp
from jax import lax
from jax.sharding import PartitionSpec as P

HEAD = 128
WINDOW = 4


def entering(part, axis, combine, identity):
    place = lax.axis_index(axis)
    gathered = jax.tree.map(lambda a: lax.all_gather(a, axis), part)
    state = jax.tree.map(lambda a, e: jnp.zeros_like(a) + jnp.asarray(e, a.dtype), part, identity)

    def one(hop, state):
        return combine(
            state, jax.tree.map(lambda a: lax.dynamic_index_in_dim(a, hop, 0, False), gathered)
        )

    return lax.fori_loop(0, place, one, state)


def from_behind(block, axis, distance):
    devices = range(lax.axis_size(axis))
    route = [(i - distance, i) for i in devices if i - distance in devices]
    return lax.ppermute(block, axis, route)


def rms_rows(values):
    widened = values.astype(jnp.float32)
    return (
        widened * lax.rsqrt(jnp.mean(widened * widened, axis=-1, keepdims=True) + 1e-05)
    ).astype(jnp.bfloat16)


def carry_last(earlier, later):
    empty = later[0] < 0
    ident = jnp.where(empty, earlier[0], later[0])
    begin_pos = jnp.where(empty | (later[0] == earlier[0]), earlier[1], later[1])
    return (ident, begin_pos)


def attend(queries, key_rows, seg_begin, query_pos, key_pos):
    row_count, head_width = queries.shape
    head_count = head_width // HEAD
    query_part = queries.reshape(row_count, head_count, HEAD)
    key_part = key_rows[:, :head_width].reshape(-1, head_count, HEAD)
    value_part = key_rows[:, head_width:].reshape(-1, head_count, HEAD)
    scores = jnp.einsum(
        "qhd,khd->hqk", query_part, key_part, preferred_element_type=jnp.float32
    ) * (1.0 / math.sqrt(HEAD))
    allowed = (key_pos[None, :] <= query_pos[:, None]) & (key_pos[None, :] >= seg_begin[:, None])
    scores = jnp.where(allowed[None], scores, -jnp.inf)
    row_top = jnp.max(scores, axis=2, keepdims=True)
    weights = jnp.exp(scores - row_top)
    weights = (weights / jnp.sum(weights, axis=2, keepdims=True)).astype(jnp.bfloat16)
    blended = jnp.einsum("hqk,khd->qhd", weights, value_part, preferred_element_type=jnp.float32)
    return blended.astype(jnp.bfloat16).reshape(row_count, head_width)


def local(inputs, segment_ids, w_query, w_keyval, w_out):
    batches = inputs.shape[0]
    row_count = inputs.shape[1]
    phase_index = lax.axis_index("phase")
    phase_count = lax.axis_size("phase")
    device = lax.axis_index("ctx")
    positions = device * row_count + jnp.arange(row_count, dtype=jnp.int32)
    before = jnp.concatenate([jnp.full((batches, 1), -1, jnp.int32), segment_ids[:, :-1]], axis=1)
    boundary = jnp.where(segment_ids != before, positions[None, :], jnp.zeros_like(segment_ids))
    local_begin = lax.cummax(boundary, axis=1)
    tail_ids = segment_ids[:, -1]
    tail_begin = local_begin[:, -1]
    prior_id, prior_begin = entering(
        (tail_ids, tail_begin),
        "ctx",
        carry_last,
        (jnp.full((batches,), -1, jnp.int32), jnp.zeros((batches,), jnp.int32)),
    )
    begins = jnp.where(segment_ids == prior_id[:, None], prior_begin[:, None], local_begin)
    keyval_full = lax.all_gather(w_keyval, "ctx", axis=1, tiled=True)[0]
    query_mat = w_query[0]
    out_mat = w_out[0]
    key_pos = (device - WINDOW + 1) * row_count + jnp.arange(WINDOW * row_count, dtype=jnp.int32)
    empty_rows = jnp.zeros((row_count, inputs.shape[2]), jnp.bfloat16)

    def tick(tick_index, carry):
        arrived, outputs = carry
        slot_raw = tick_index - phase_index
        active = (slot_raw >= 0) & (slot_raw < batches)
        slot_index = jnp.clip(slot_raw, 0, batches - 1)
        loaded = lax.dynamic_index_in_dim(inputs, slot_index, 0, keepdims=False)
        stream = jnp.where(phase_index == 0, loaded, arrived)
        normed = rms_rows(stream)
        queries = jnp.dot(normed, query_mat, preferred_element_type=jnp.float32).astype(
            jnp.bfloat16
        )
        keyvals = jnp.dot(normed, keyval_full, preferred_element_type=jnp.float32).astype(
            jnp.bfloat16
        )
        seg_begin = lax.dynamic_index_in_dim(begins, slot_index, 0, keepdims=False)
        earlier = []
        for offset in range(WINDOW - 1, 0, -1):
            earlier.append(from_behind(keyvals, "ctx", offset))
        key_rows = jnp.concatenate(earlier + [keyvals], axis=0)
        blended = attend(queries, key_rows, seg_begin, positions, key_pos)
        update = jnp.dot(blended, out_mat, preferred_element_type=jnp.float32)
        result = (stream.astype(jnp.float32) + update).astype(jnp.bfloat16)
        previous = lax.dynamic_index_in_dim(outputs, slot_index, 0, keepdims=False)
        written = jnp.where(active, result, previous)
        outputs = lax.dynamic_update_index_in_dim(outputs, written, slot_index, 0)
        arrived = from_behind(result, "phase", 1)
        return (arrived, outputs)

    tick_count = batches + phase_count - 1
    outputs = jnp.zeros((batches, row_count, inputs.shape[2]), jnp.bfloat16)
    arrived, outputs = lax.fori_loop(0, tick_count, tick, (empty_rows, outputs))
    return outputs[None]


def solution(mesh):
    placed = (
        P(None, "ctx", None),
        P(None, "ctx"),
        P("phase", None, None),
        P("phase", "ctx", None),
        P("phase", None, None),
    )
    return jax.shard_map(
        local, mesh=mesh, in_specs=placed, out_specs=P("phase", None, "ctx", None), check_vma=False
    )
```

profile of v0, /device:TPU:63, one launch (start us, length us, event | category | flops | bytes accessed | tf_op | source)
XLA Modules:
  0.0 830.7 jit_solution(16806175467223868526)
XLA Ops:
  14.3 14.7 %all-reduce.2 = (s32[32]{0:T(128)S(1)}, s32[32]{0:T(128)S(1)}) all-reduce(s32[32]{0:T(128)S(1)} %bitcast_dynamic-update-slice_fusion.1, s32[32]{0:T(128)S(1)} %bitcast_dynamic-update-slice_fusion), channel_id=1, replica_groups=mesh['phase'=8,'ctx'=32] {'ctx'}, use_global_device_ids=true, to_apply=%add | all-reduce | flops 64 | bytes 512
  29.0 81.3 %while.29 = (s32[]{:T(128)}, s32[1]{0:T(128)}, s32[1]{0:T(128)}, s32[]{:T(128)}, s32[32,1]{0,1:T(1,128)S(1)}, /*index=5*/s32[32,1]{0,1:T(1,128)S(1)}, s32[]{:T(128)}, s32[]{:T(128)}, s32[]{:T(128)}, s32[1]{0:T(128)}) while((s32[]{:T(128)}, s32[1]{0:T(128)}, s32[1]{0:T(128)}, s32[]{:T(128)}, s32[32,1]{0,1:T(1,128)S(1)}, ...), condition=%wide.region_2.3_spmd, body=%wide.region_1.2_spmd.sunk | while | flops 10 | bytes 202 | solution.py:22
  111.9 711.1 %while.30 = (s32[]{:T(128)}, bf16[128,2048]{1,0:T(8,128)(2,1)}, bf16[1,128,2048]{2,1,0:T(8,128)(2,1)S(1)}, pred[]{:T(512)}, bf16[1,128,2048]{2,1,0:T(8,128)(2,1)...) while((s32[]{:T(128)}, bf16[128,2048]{1,0:T(8,128)(2,1)}, ...), condition=%wide.region_7.8_spmd.clone, body=%wide.region_3.7_spmd.clone.sunk | while | flops 2431845632 | bytes 82461064 | solution.py:118
  118.3 10.2 %collective-permute-start = (bf16[128,2048]{1,0:T(8,128)(2,1)S(1)}, bf16[128,2048]{1,0:T(8,128)(2,1)S(1)}, u32[]{:S(2)}, u32[]{:S(2)}) collective-permute-start(bf16[128,2048]{1,0:T(8,128)(2,1)S(1)} %convolution_convert_fusion.5), channel_id=1, source_target_pairs={{0,1},{1,2},{2,3},{3,4},{4,5},{5,6},{6,7},{7,8},{8,9},{9,10},{10,1... | collective-permute-start | bytes 1572872 | tf_op jit(solution)/shard_map/while/body/eval_jaxpr/ppermute | solution.py:28
  128.5 8.6 %collective-permute-start.1 = (bf16[128,2048]{1,0:T(8,128)(2,1)S(1)}, bf16[128,2048]{1,0:T(8,128)(2,1)S(1)}, u32[]{:S(2)}, u32[]{:S(2)}) collective-permute-start(bf16[128,2048]{1,0:T(8,128)(2,1)S(1)} %convolution_convert_fusion.5), channel_id=1, source_target_pairs={{0,2},{1,3},{2,4},{3,5},{4,6},{5,7},{6,8},{7,9},{8,10},{9,11},{10,... | collective-permute-start | bytes 1572872 | tf_op jit(solution)/shard_map/while/body/eval_jaxpr/ppermute | solution.py:28
  137.1 10.2 %collective-permute-start.2 = (bf16[128,2048]{1,0:T(8,128)(2,1)S(1)}, bf16[128,2048]{1,0:T(8,128)(2,1)S(1)}, u32[]{:S(2)}, u32[]{:S(2)}) collective-permute-start(bf16[128,2048]{1,0:T(8,128)(2,1)S(1)} %convolution_convert_fusion.5), channel_id=1, source_target_pairs={{0,3},{1,4},{2,5},{3,6},{4,7},{5,8},{6,9},{7,10},{8,11},{9,12},{10... | collective-permute-start | bytes 1572872 | tf_op jit(solution)/shard_map/while/body/eval_jaxpr/ppermute | solution.py:28
  148.3 19.3 %collective-permute-done = bf16[128,2048]{1,0:T(8,128)(2,1)S(1)} collective-permute-done((bf16[128,2048]{1,0:T(8,128)(2,1)S(1)}, bf16[128,2048]{1,0:T(8,128)(2,1)S(1)}, u32[]{:S(2)}, u32[]{:S(2)}) %collective-permute-start) | collective-permute-done | bytes 524320 | tf_op jit(solution)/shard_map/while/body/eval_jaxpr/ppermute | solution.py:28
  167.6 11.2 %collective-permute-done.1 = bf16[128,2048]{1,0:T(8,128)(2,1)S(1)} collective-permute-done((bf16[128,2048]{1,0:T(8,128)(2,1)S(1)}, bf16[128,2048]{1,0:T(8,128)(2,1)S(1)}, u32[]{:S(2)}, u32[]{:S(2)}) %collective-permute-start.1) | collective-permute-done | bytes 524320 | tf_op jit(solution)/shard_map/while/body/eval_jaxpr/ppermute | solution.py:28
  193.7 11.4 %collective-permute-done.3 = bf16[128,2048]{1,0:T(8,128)(2,1)} collective-permute-done((bf16[128,2048]{1,0:T(8,128)(2,1)S(1)}, bf16[128,2048]{1,0:T(8,128)(2,1)}, u32[]{:S(2)}, u32[]{:S(2)}) %collective-permute-start.3) | collective-permute-done | bytes 524320 | tf_op jit(solution)/shard_map/while/body/eval_jaxpr/ppermute | solution.py:28
  211.4 9.2 %collective-permute-start = (bf16[128,2048]{1,0:T(8,128)(2,1)S(1)}, bf16[128,2048]{1,0:T(8,128)(2,1)S(1)}, u32[]{:S(2)}, u32[]{:S(2)}) collective-permute-start(bf16[128,2048]{1,0:T(8,128)(2,1)S(1)} %convolution_convert_fusion.5), channel_id=1, source_target_pairs={{0,1},{1,2},{2,3},{3,4},{4,5},{5,6},{6,7},{7,8},{8,9},{9,10},{10,1... | collective-permute-start | bytes 1572872 | tf_op jit(solution)/shard_map/while/body/eval_jaxpr/ppermute | solution.py:28
  228.1 30.2 %collective-permute-done = bf16[128,2048]{1,0:T(8,128)(2,1)S(1)} collective-permute-done((bf16[128,2048]{1,0:T(8,128)(2,1)S(1)}, bf16[128,2048]{1,0:T(8,128)(2,1)S(1)}, u32[]{:S(2)}, u32[]{:S(2)}) %collective-permute-start) | collective-permute-done | bytes 524320 | tf_op jit(solution)/shard_map/while/body/eval_jaxpr/ppermute | solution.py:28
  258.3 14.2 %collective-permute-done.1 = bf16[128,2048]{1,0:T(8,128)(2,1)S(1)} collective-permute-done((bf16[128,2048]{1,0:T(8,128)(2,1)S(1)}, bf16[128,2048]{1,0:T(8,128)(2,1)S(1)}, u32[]{:S(2)}, u32[]{:S(2)}) %collective-permute-start.1) | collective-permute-done | bytes 524320 | tf_op jit(solution)/shard_map/while/body/eval_jaxpr/ppermute | solution.py:28
  283.0 14.5 %collective-permute-done.3 = bf16[128,2048]{1,0:T(8,128)(2,1)} collective-permute-done((bf16[128,2048]{1,0:T(8,128)(2,1)S(1)}, bf16[128,2048]{1,0:T(8,128)(2,1)}, u32[]{:S(2)}, u32[]{:S(2)}) %collective-permute-start.3) | collective-permute-done | bytes 524320 | tf_op jit(solution)/shard_map/while/body/eval_jaxpr/ppermute | solution.py:28
  310.6 34.0 %collective-permute-done = bf16[128,2048]{1,0:T(8,128)(2,1)S(1)} collective-permute-done((bf16[128,2048]{1,0:T(8,128)(2,1)S(1)}, bf16[128,2048]{1,0:T(8,128)(2,1)S(1)}, u32[]{:S(2)}, u32[]{:S(2)}) %collective-permute-start) | collective-permute-done | bytes 524320 | tf_op jit(solution)/shard_map/while/body/eval_jaxpr/ppermute | solution.py:28
  344.5 11.2 %collective-permute-done.1 = bf16[128,2048]{1,0:T(8,128)(2,1)S(1)} collective-permute-done((bf16[128,2048]{1,0:T(8,128)(2,1)S(1)}, bf16[128,2048]{1,0:T(8,128)(2,1)S(1)}, u32[]{:S(2)}, u32[]{:S(2)}) %collective-permute-start.1) | collective-permute-done | bytes 524320 | tf_op jit(solution)/shard_map/while/body/eval_jaxpr/ppermute | solution.py:28
  355.8 7.5 collective-permute-done.2
  373.7 8.6 %collective-permute-done.3 = bf16[128,2048]{1,0:T(8,128)(2,1)} collective-permute-done((bf16[128,2048]{1,0:T(8,128)(2,1)S(1)}, bf16[128,2048]{1,0:T(8,128)(2,1)}, u32[]{:S(2)}, u32[]{:S(2)}) %collective-permute-start.3) | collective-permute-done | bytes 524320 | tf_op jit(solution)/shard_map/while/body/eval_jaxpr/ppermute | solution.py:28
  395.4 32.5 %collective-permute-done = bf16[128,2048]{1,0:T(8,128)(2,1)S(1)} collective-permute-done((bf16[128,2048]{1,0:T(8,128)(2,1)S(1)}, bf16[128,2048]{1,0:T(8,128)(2,1)S(1)}, u32[]{:S(2)}, u32[]{:S(2)}) %collective-permute-start) | collective-permute-done | bytes 524320 | tf_op jit(solution)/shard_map/while/body/eval_jaxpr/ppermute | solution.py:28
  427.9 11.2 %collective-permute-done.1 = bf16[128,2048]{1,0:T(8,128)(2,1)S(1)} collective-permute-done((bf16[128,2048]{1,0:T(8,128)(2,1)S(1)}, bf16[128,2048]{1,0:T(8,128)(2,1)S(1)}, u32[]{:S(2)}, u32[]{:S(2)}) %collective-permute-start.1) | collective-permute-done | bytes 524320 | tf_op jit(solution)/shard_map/while/body/eval_jaxpr/ppermute | solution.py:28
  449.5 17.7 %collective-permute-done.3 = bf16[128,2048]{1,0:T(8,128)(2,1)} collective-permute-done((bf16[128,2048]{1,0:T(8,128)(2,1)S(1)}, bf16[128,2048]{1,0:T(8,128)(2,1)}, u32[]{:S(2)}, u32[]{:S(2)}) %collective-permute-start.3) | collective-permute-done | bytes 524320 | tf_op jit(solution)/shard_map/while/body/eval_jaxpr/ppermute | solution.py:28
  484.6 45.2 %collective-permute-done.1 = bf16[128,2048]{1,0:T(8,128)(2,1)S(1)} collective-permute-done((bf16[128,2048]{1,0:T(8,128)(2,1)S(1)}, bf16[128,2048]{1,0:T(8,128)(2,1)S(1)}, u32[]{:S(2)}, u32[]{:S(2)}) %collective-permute-start.1) | collective-permute-done | bytes 524320 | tf_op jit(solution)/shard_map/while/body/eval_jaxpr/ppermute | solution.py:28
  544.1 8.6 %collective-permute-done.3 = bf16[128,2048]{1,0:T(8,128)(2,1)} collective-permute-done((bf16[128,2048]{1,0:T(8,128)(2,1)S(1)}, bf16[128,2048]{1,0:T(8,128)(2,1)}, u32[]{:S(2)}, u32[]{:S(2)}) %collective-permute-start.3) | collective-permute-done | bytes 524320 | tf_op jit(solution)/shard_map/while/body/eval_jaxpr/ppermute | solution.py:28
  565.8 21.2 %collective-permute-done = bf16[128,2048]{1,0:T(8,128)(2,1)S(1)} collective-permute-done((bf16[128,2048]{1,0:T(8,128)(2,1)S(1)}, bf16[128,2048]{1,0:T(8,128)(2,1)S(1)}, u32[]{:S(2)}, u32[]{:S(2)}) %collective-permute-start) | collective-permute-done | bytes 524320 | tf_op jit(solution)/shard_map/while/body/eval_jaxpr/ppermute | solution.py:28
  586.9 22.6 %collective-permute-done.1 = bf16[128,2048]{1,0:T(8,128)(2,1)S(1)} collective-permute-done((bf16[128,2048]{1,0:T(8,128)(2,1)S(1)}, bf16[128,2048]{1,0:T(8,128)(2,1)S(1)}, u32[]{:S(2)}, u32[]{:S(2)}) %collective-permute-start.1) | collective-permute-done | bytes 524320 | tf_op jit(solution)/shard_map/while/body/eval_jaxpr/ppermute | solution.py:28
  619.9 24.5 %collective-permute-done.3 = bf16[128,2048]{1,0:T(8,128)(2,1)} collective-permute-done((bf16[128,2048]{1,0:T(8,128)(2,1)S(1)}, bf16[128,2048]{1,0:T(8,128)(2,1)}, u32[]{:S(2)}, u32[]{:S(2)}) %collective-permute-start.3) | collective-permute-done | bytes 524320 | tf_op jit(solution)/shard_map/while/body/eval_jaxpr/ppermute | solution.py:28
  657.5 32.5 %collective-permute-done = bf16[128,2048]{1,0:T(8,128)(2,1)S(1)} collective-permute-done((bf16[128,2048]{1,0:T(8,128)(2,1)S(1)}, bf16[128,2048]{1,0:T(8,128)(2,1)S(1)}, u32[]{:S(2)}, u32[]{:S(2)}) %collective-permute-start) | collective-permute-done | bytes 524320 | tf_op jit(solution)/shard_map/while/body/eval_jaxpr/ppermute | solution.py:28
  690.0 11.2 %collective-permute-done.1 = bf16[128,2048]{1,0:T(8,128)(2,1)S(1)} collective-permute-done((bf16[128,2048]{1,0:T(8,128)(2,1)S(1)}, bf16[128,2048]{1,0:T(8,128)(2,1)S(1)}, u32[]{:S(2)}, u32[]{:S(2)}) %collective-permute-start.1) | collective-permute-done | bytes 524320 | tf_op jit(solution)/shard_map/while/body/eval_jaxpr/ppermute | solution.py:28
  701.2 10.8 %collective-permute-done.2 = bf16[128,2048]{1,0:T(8,128)(2,1)S(1)} collective-permute-done((bf16[128,2048]{1,0:T(8,128)(2,1)S(1)}, bf16[128,2048]{1,0:T(8,128)(2,1)S(1)}, u32[]{:S(2)}, u32[]{:S(2)}) %collective-permute-start.2) | collective-permute-done | bytes 524320 | tf_op jit(solution)/shard_map/while/body/eval_jaxpr/ppermute | solution.py:28
  722.4 8.6 %collective-permute-done.3 = bf16[128,2048]{1,0:T(8,128)(2,1)} collective-permute-done((bf16[128,2048]{1,0:T(8,128)(2,1)S(1)}, bf16[128,2048]{1,0:T(8,128)(2,1)}, u32[]{:S(2)}, u32[]{:S(2)}) %collective-permute-start.3) | collective-permute-done | bytes 524320 | tf_op jit(solution)/shard_map/while/body/eval_jaxpr/ppermute | solution.py:28
  744.1 32.5 %collective-permute-done = bf16[128,2048]{1,0:T(8,128)(2,1)S(1)} collective-permute-done((bf16[128,2048]{1,0:T(8,128)(2,1)S(1)}, bf16[128,2048]{1,0:T(8,128)(2,1)S(1)}, u32[]{:S(2)}, u32[]{:S(2)}) %collective-permute-start) | collective-permute-done | bytes 524320 | tf_op jit(solution)/shard_map/while/body/eval_jaxpr/ppermute | solution.py:28
  776.5 20.5 %collective-permute-done.1 = bf16[128,2048]{1,0:T(8,128)(2,1)S(1)} collective-permute-done((bf16[128,2048]{1,0:T(8,128)(2,1)S(1)}, bf16[128,2048]{1,0:T(8,128)(2,1)S(1)}, u32[]{:S(2)}, u32[]{:S(2)}) %collective-permute-start.1) | collective-permute-done | bytes 524320 | tf_op jit(solution)/shard_map/while/body/eval_jaxpr/ppermute | solution.py:28
  814.5 8.6 %collective-permute-done.3 = bf16[128,2048]{1,0:T(8,128)(2,1)} collective-permute-done((bf16[128,2048]{1,0:T(8,128)(2,1)S(1)}, bf16[128,2048]{1,0:T(8,128)(2,1)}, u32[]{:S(2)}, u32[]{:S(2)}) %collective-permute-start.3) | collective-permute-done | bytes 524320 | tf_op jit(solution)/shard_map/while/body/eval_jaxpr/ppermute | solution.py:28
  (221 shorter events, 228.1 us)
Async XLA Ops:
  6.5 104.4 %all-gather.2.cloned.1.call-start = ((), (), s32[]{:S(2)}) async-start(), calls=%async_computation | async-start | bytes 8650752 | tf_op jit(solution)/shard_map/all_gather | solution.py:82
  118.3 49.3 %collective-permute-start = (bf16[128,2048]{1,0:T(8,128)(2,1)S(1)}, bf16[128,2048]{1,0:T(8,128)(2,1)S(1)}, u32[]{:S(2)}, u32[]{:S(2)}) collective-permute-start(bf16[128,2048]{1,0:T(8,128)(2,1)S(1)} %convolution_convert_fusion.5), channel_id=1, source_target_pairs={{0,1},{1,2},{2,3},{3,4},{4,5},{5,6},{6,7},{7,8},{8,9},{9,10},{10,1... | collective-permute-start | bytes 1572872 | tf_op jit(solution)/shard_map/while/body/eval_jaxpr/ppermute | solution.py:28
  128.5 50.3 %collective-permute-start.1 = (bf16[128,2048]{1,0:T(8,128)(2,1)S(1)}, bf16[128,2048]{1,0:T(8,128)(2,1)S(1)}, u32[]{:S(2)}, u32[]{:S(2)}) collective-permute-start(bf16[128,2048]{1,0:T(8,128)(2,1)S(1)} %convolution_convert_fusion.5), channel_id=1, source_target_pairs={{0,2},{1,3},{2,4},{3,5},{4,6},{5,7},{6,8},{7,9},{8,10},{9,11},{10,... | collective-permute-start | bytes 1572872 | tf_op jit(solution)/shard_map/while/body/eval_jaxpr/ppermute | solution.py:28
  137.1 46.1 %collective-permute-start.2 = (bf16[128,2048]{1,0:T(8,128)(2,1)S(1)}, bf16[128,2048]{1,0:T(8,128)(2,1)S(1)}, u32[]{:S(2)}, u32[]{:S(2)}) collective-permute-start(bf16[128,2048]{1,0:T(8,128)(2,1)S(1)} %convolution_convert_fusion.5), channel_id=1, source_target_pairs={{0,3},{1,4},{2,5},{3,6},{4,7},{5,8},{6,9},{7,10},{8,11},{9,12},{10... | collective-permute-start | bytes 1572872 | tf_op jit(solution)/shard_map/while/body/eval_jaxpr/ppermute | solution.py:28
  192.2 12.8 %collective-permute-start.3 = (bf16[128,2048]{1,0:T(8,128)(2,1)S(1)}, bf16[128,2048]{1,0:T(8,128)(2,1)}, u32[]{:S(2)}, u32[]{:S(2)}) collective-permute-start(bf16[128,2048]{1,0:T(8,128)(2,1)S(1)} %fusion.71), channel_id=1, source_target_pairs={{0,32},{32,64},{64,96},{96,128},{128,160},{160,192},{192,224},{1,3... | collective-permute-start | bytes 1572872 | tf_op jit(solution)/shard_map/while/body/eval_jaxpr/ppermute | solution.py:28
  211.4 46.9 %collective-permute-start = (bf16[128,2048]{1,0:T(8,128)(2,1)S(1)}, bf16[128,2048]{1,0:T(8,128)(2,1)S(1)}, u32[]{:S(2)}, u32[]{:S(2)}) collective-permute-start(bf16[128,2048]{1,0:T(8,128)(2,1)S(1)} %convolution_convert_fusion.5), channel_id=1, source_target_pairs={{0,1},{1,2},{2,3},{3,4},{4,5},{5,6},{6,7},{7,8},{8,9},{9,10},{10,1... | collective-permute-start | bytes 1572872 | tf_op jit(solution)/shard_map/while/body/eval_jaxpr/ppermute | solution.py:28
  220.6 51.9 %collective-permute-start.1 = (bf16[128,2048]{1,0:T(8,128)(2,1)S(1)}, bf16[128,2048]{1,0:T(8,128)(2,1)S(1)}, u32[]{:S(2)}, u32[]{:S(2)}) collective-permute-start(bf16[128,2048]{1,0:T(8,128)(2,1)S(1)} %convolution_convert_fusion.5), channel_id=1, source_target_pairs={{0,2},{1,3},{2,4},{3,5},{4,6},{5,7},{6,8},{7,9},{8,10},{9,11},{10,... | collective-permute-start | bytes 1572872 | tf_op jit(solution)/shard_map/while/body/eval_jaxpr/ppermute | solution.py:28
  222.5 50.1 %collective-permute-start.2 = (bf16[128,2048]{1,0:T(8,128)(2,1)S(1)}, bf16[128,2048]{1,0:T(8,128)(2,1)S(1)}, u32[]{:S(2)}, u32[]{:S(2)}) collective-permute-start(bf16[128,2048]{1,0:T(8,128)(2,1)S(1)} %convolution_convert_fusion.5), channel_id=1, source_target_pairs={{0,3},{1,4},{2,5},{3,6},{4,7},{5,8},{6,9},{7,10},{8,11},{9,12},{10... | collective-permute-start | bytes 1572872 | tf_op jit(solution)/shard_map/while/body/eval_jaxpr/ppermute | solution.py:28
  281.6 15.9 %collective-permute-start.3 = (bf16[128,2048]{1,0:T(8,128)(2,1)S(1)}, bf16[128,2048]{1,0:T(8,128)(2,1)}, u32[]{:S(2)}, u32[]{:S(2)}) collective-permute-start(bf16[128,2048]{1,0:T(8,128)(2,1)S(1)} %fusion.71), channel_id=1, source_target_pairs={{0,32},{32,64},{64,96},{96,128},{128,160},{160,192},{192,224},{1,3... | collective-permute-start | bytes 1572872 | tf_op jit(solution)/shard_map/while/body/eval_jaxpr/ppermute | solution.py:28
  303.8 40.7 %collective-permute-start = (bf16[128,2048]{1,0:T(8,128)(2,1)S(1)}, bf16[128,2048]{1,0:T(8,128)(2,1)S(1)}, u32[]{:S(2)}, u32[]{:S(2)}) collective-permute-start(bf16[128,2048]{1,0:T(8,128)(2,1)S(1)} %convolution_convert_fusion.5), channel_id=1, source_target_pairs={{0,1},{1,2},{2,3},{3,4},{4,5},{5,6},{6,7},{7,8},{8,9},{9,10},{10,1... | collective-permute-start | bytes 1572872 | tf_op jit(solution)/shard_map/while/body/eval_jaxpr/ppermute | solution.py:28
  305.8 50.0 %collective-permute-start.1 = (bf16[128,2048]{1,0:T(8,128)(2,1)S(1)}, bf16[128,2048]{1,0:T(8,128)(2,1)S(1)}, u32[]{:S(2)}, u32[]{:S(2)}) collective-permute-start(bf16[128,2048]{1,0:T(8,128)(2,1)S(1)} %convolution_convert_fusion.5), channel_id=1, source_target_pairs={{0,2},{1,3},{2,4},{3,5},{4,6},{5,7},{6,8},{7,9},{8,10},{9,11},{10,... | collective-permute-start | bytes 1572872 | tf_op jit(solution)/shard_map/while/body/eval_jaxpr/ppermute | solution.py:28
  307.7 55.6 %collective-permute-start.2 = (bf16[128,2048]{1,0:T(8,128)(2,1)S(1)}, bf16[128,2048]{1,0:T(8,128)(2,1)S(1)}, u32[]{:S(2)}, u32[]{:S(2)}) collective-permute-start(bf16[128,2048]{1,0:T(8,128)(2,1)S(1)} %convolution_convert_fusion.5), channel_id=1, source_target_pairs={{0,3},{1,4},{2,5},{3,6},{4,7},{5,8},{6,9},{7,10},{8,11},{9,12},{10... | collective-permute-start | bytes 1572872 | tf_op jit(solution)/shard_map/while/body/eval_jaxpr/ppermute | solution.py:28
  372.2 10.1 %collective-permute-start.3 = (bf16[128,2048]{1,0:T(8,128)(2,1)S(1)}, bf16[128,2048]{1,0:T(8,128)(2,1)}, u32[]{:S(2)}, u32[]{:S(2)}) collective-permute-start(bf16[128,2048]{1,0:T(8,128)(2,1)S(1)} %fusion.71), channel_id=1, source_target_pairs={{0,32},{32,64},{64,96},{96,128},{128,160},{160,192},{192,224},{1,3... | collective-permute-start | bytes 1572872 | tf_op jit(solution)/shard_map/while/body/eval_jaxpr/ppermute | solution.py:28
  388.6 39.2 %collective-permute-start = (bf16[128,2048]{1,0:T(8,128)(2,1)S(1)}, bf16[128,2048]{1,0:T(8,128)(2,1)S(1)}, u32[]{:S(2)}, u32[]{:S(2)}) collective-permute-start(bf16[128,2048]{1,0:T(8,128)(2,1)S(1)} %convolution_convert_fusion.5), channel_id=1, source_target_pairs={{0,1},{1,2},{2,3},{3,4},{4,5},{5,6},{6,7},{7,8},{8,9},{9,10},{10,1... | collective-permute-start | bytes 1572872 | tf_op jit(solution)/shard_map/while/body/eval_jaxpr/ppermute | solution.py:28
  390.6 48.5 %collective-permute-start.1 = (bf16[128,2048]{1,0:T(8,128)(2,1)S(1)}, bf16[128,2048]{1,0:T(8,128)(2,1)S(1)}, u32[]{:S(2)}, u32[]{:S(2)}) collective-permute-start(bf16[128,2048]{1,0:T(8,128)(2,1)S(1)} %convolution_convert_fusion.5), channel_id=1, source_target_pairs={{0,2},{1,3},{2,4},{3,5},{4,6},{5,7},{6,8},{7,9},{8,10},{9,11},{10,... | collective-permute-start | bytes 1572872 | tf_op jit(solution)/shard_map/while/body/eval_jaxpr/ppermute | solution.py:28
  392.5 46.6 %collective-permute-start.2 = (bf16[128,2048]{1,0:T(8,128)(2,1)S(1)}, bf16[128,2048]{1,0:T(8,128)(2,1)S(1)}, u32[]{:S(2)}, u32[]{:S(2)}) collective-permute-start(bf16[128,2048]{1,0:T(8,128)(2,1)S(1)} %convolution_convert_fusion.5), channel_id=1, source_target_pairs={{0,3},{1,4},{2,5},{3,6},{4,7},{5,8},{6,9},{7,10},{8,11},{9,12},{10... | collective-permute-start | bytes 1572872 | tf_op jit(solution)/shard_map/while/body/eval_jaxpr/ppermute | solution.py:28
  448.1 19.1 %collective-permute-start.3 = (bf16[128,2048]{1,0:T(8,128)(2,1)S(1)}, bf16[128,2048]{1,0:T(8,128)(2,1)}, u32[]{:S(2)}, u32[]{:S(2)}) collective-permute-start(bf16[128,2048]{1,0:T(8,128)(2,1)S(1)} %fusion.71), channel_id=1, source_target_pairs={{0,32},{32,64},{64,96},{96,128},{128,160},{160,192},{192,224},{1,3... | collective-permute-start | bytes 1572872 | tf_op jit(solution)/shard_map/while/body/eval_jaxpr/ppermute | solution.py:28
  473.5 11.1 %collective-permute-start = (bf16[128,2048]{1,0:T(8,128)(2,1)S(1)}, bf16[128,2048]{1,0:T(8,128)(2,1)S(1)}, u32[]{:S(2)}, u32[]{:S(2)}) collective-permute-start(bf16[128,2048]{1,0:T(8,128)(2,1)S(1)} %convolution_convert_fusion.5), channel_id=1, source_target_pairs={{0,1},{1,2},{2,3},{3,4},{4,5},{5,6},{6,7},{7,8},{8,9},{9,10},{10,1... | collective-permute-start | bytes 1572872 | tf_op jit(solution)/shard_map/while/body/eval_jaxpr/ppermute | solution.py:28
  475.4 54.4 %collective-permute-start.1 = (bf16[128,2048]{1,0:T(8,128)(2,1)S(1)}, bf16[128,2048]{1,0:T(8,128)(2,1)S(1)}, u32[]{:S(2)}, u32[]{:S(2)}) collective-permute-start(bf16[128,2048]{1,0:T(8,128)(2,1)S(1)} %convolution_convert_fusion.5), channel_id=1, source_target_pairs={{0,2},{1,3},{2,4},{3,5},{4,6},{5,7},{6,8},{7,9},{8,10},{9,11},{10,... | collective-permute-start | bytes 1572872 | tf_op jit(solution)/shard_map/while/body/eval_jaxpr/ppermute | solution.py:28
  477.4 56.3 %collective-permute-start.2 = (bf16[128,2048]{1,0:T(8,128)(2,1)S(1)}, bf16[128,2048]{1,0:T(8,128)(2,1)S(1)}, u32[]{:S(2)}, u32[]{:S(2)}) collective-permute-start(bf16[128,2048]{1,0:T(8,128)(2,1)S(1)} %convolution_convert_fusion.5), channel_id=1, source_target_pairs={{0,3},{1,4},{2,5},{3,6},{4,7},{5,8},{6,9},{7,10},{8,11},{9,12},{10... | collective-permute-start | bytes 1572872 | tf_op jit(solution)/shard_map/while/body/eval_jaxpr/ppermute | solution.py:28
  542.7 10.0 %collective-permute-start.3 = (bf16[128,2048]{1,0:T(8,128)(2,1)S(1)}, bf16[128,2048]{1,0:T(8,128)(2,1)}, u32[]{:S(2)}, u32[]{:S(2)}) collective-permute-start(bf16[128,2048]{1,0:T(8,128)(2,1)S(1)} %fusion.71), channel_id=1, source_target_pairs={{0,32},{32,64},{64,96},{96,128},{128,160},{160,192},{192,224},{1,3... | collective-permute-start | bytes 1572872 | tf_op jit(solution)/shard_map/while/body/eval_jaxpr/ppermute | solution.py:28
  559.0 27.9 %collective-permute-start = (bf16[128,2048]{1,0:T(8,128)(2,1)S(1)}, bf16[128,2048]{1,0:T(8,128)(2,1)S(1)}, u32[]{:S(2)}, u32[]{:S(2)}) collective-permute-start(bf16[128,2048]{1,0:T(8,128)(2,1)S(1)} %convolution_convert_fusion.5), channel_id=1, source_target_pairs={{0,1},{1,2},{2,3},{3,4},{4,5},{5,6},{6,7},{7,8},{8,9},{9,10},{10,1... | collective-permute-start | bytes 1572872 | tf_op jit(solution)/shard_map/while/body/eval_jaxpr/ppermute | solution.py:28
  560.9 48.6 %collective-permute-start.1 = (bf16[128,2048]{1,0:T(8,128)(2,1)S(1)}, bf16[128,2048]{1,0:T(8,128)(2,1)S(1)}, u32[]{:S(2)}, u32[]{:S(2)}) collective-permute-start(bf16[128,2048]{1,0:T(8,128)(2,1)S(1)} %convolution_convert_fusion.5), channel_id=1, source_target_pairs={{0,2},{1,3},{2,4},{3,5},{4,6},{5,7},{6,8},{7,9},{8,10},{9,11},{10,... | collective-permute-start | bytes 1572872 | tf_op jit(solution)/shard_map/while/body/eval_jaxpr/ppermute | solution.py:28
  562.9 46.6 %collective-permute-start.2 = (bf16[128,2048]{1,0:T(8,128)(2,1)S(1)}, bf16[128,2048]{1,0:T(8,128)(2,1)S(1)}, u32[]{:S(2)}, u32[]{:S(2)}) collective-permute-start(bf16[128,2048]{1,0:T(8,128)(2,1)S(1)} %convolution_convert_fusion.5), channel_id=1, source_target_pairs={{0,3},{1,4},{2,5},{3,6},{4,7},{5,8},{6,9},{7,10},{8,11},{9,12},{10... | collective-permute-start | bytes 1572872 | tf_op jit(solution)/shard_map/while/body/eval_jaxpr/ppermute | solution.py:28
  618.5 26.0 %collective-permute-start.3 = (bf16[128,2048]{1,0:T(8,128)(2,1)S(1)}, bf16[128,2048]{1,0:T(8,128)(2,1)}, u32[]{:S(2)}, u32[]{:S(2)}) collective-permute-start(bf16[128,2048]{1,0:T(8,128)(2,1)S(1)} %fusion.71), channel_id=1, source_target_pairs={{0,32},{32,64},{64,96},{96,128},{128,160},{160,192},{192,224},{1,3... | collective-permute-start | bytes 1572872 | tf_op jit(solution)/shard_map/while/body/eval_jaxpr/ppermute | solution.py:28
  650.8 39.2 %collective-permute-start = (bf16[128,2048]{1,0:T(8,128)(2,1)S(1)}, bf16[128,2048]{1,0:T(8,128)(2,1)S(1)}, u32[]{:S(2)}, u32[]{:S(2)}) collective-permute-start(bf16[128,2048]{1,0:T(8,128)(2,1)S(1)} %convolution_convert_fusion.5), channel_id=1, source_target_pairs={{0,1},{1,2},{2,3},{3,4},{4,5},{5,6},{6,7},{7,8},{8,9},{9,10},{10,1... | collective-permute-start | bytes 1572872 | tf_op jit(solution)/shard_map/while/body/eval_jaxpr/ppermute | solution.py:28
  652.7 48.5 %collective-permute-start.1 = (bf16[128,2048]{1,0:T(8,128)(2,1)S(1)}, bf16[128,2048]{1,0:T(8,128)(2,1)S(1)}, u32[]{:S(2)}, u32[]{:S(2)}) collective-permute-start(bf16[128,2048]{1,0:T(8,128)(2,1)S(1)} %convolution_convert_fusion.5), channel_id=1, source_target_pairs={{0,2},{1,3},{2,4},{3,5},{4,6},{5,7},{6,8},{7,9},{8,10},{9,11},{10,... | collective-permute-start | bytes 1572872 | tf_op jit(solution)/shard_map/while/body/eval_jaxpr/ppermute | solution.py:28
  654.6 57.3 %collective-permute-start.2 = (bf16[128,2048]{1,0:T(8,128)(2,1)S(1)}, bf16[128,2048]{1,0:T(8,128)(2,1)S(1)}, u32[]{:S(2)}, u32[]{:S(2)}) collective-permute-start(bf16[128,2048]{1,0:T(8,128)(2,1)S(1)} %convolution_convert_fusion.5), channel_id=1, source_target_pairs={{0,3},{1,4},{2,5},{3,6},{4,7},{5,8},{6,9},{7,10},{8,11},{9,12},{10... | collective-permute-start | bytes 1572872 | tf_op jit(solution)/shard_map/while/body/eval_jaxpr/ppermute | solution.py:28
  721.0 10.0 %collective-permute-start.3 = (bf16[128,2048]{1,0:T(8,128)(2,1)S(1)}, bf16[128,2048]{1,0:T(8,128)(2,1)}, u32[]{:S(2)}, u32[]{:S(2)}) collective-permute-start(bf16[128,2048]{1,0:T(8,128)(2,1)S(1)} %fusion.71), channel_id=1, source_target_pairs={{0,32},{32,64},{64,96},{96,128},{128,160},{160,192},{192,224},{1,3... | collective-permute-start | bytes 1572872 | tf_op jit(solution)/shard_map/while/body/eval_jaxpr/ppermute | solution.py:28
  737.3 39.2 %collective-permute-start = (bf16[128,2048]{1,0:T(8,128)(2,1)S(1)}, bf16[128,2048]{1,0:T(8,128)(2,1)S(1)}, u32[]{:S(2)}, u32[]{:S(2)}) collective-permute-start(bf16[128,2048]{1,0:T(8,128)(2,1)S(1)} %convolution_convert_fusion.5), channel_id=1, source_target_pairs={{0,1},{1,2},{2,3},{3,4},{4,5},{5,6},{6,7},{7,8},{8,9},{9,10},{10,1... | collective-permute-start | bytes 1572872 | tf_op jit(solution)/shard_map/while/body/eval_jaxpr/ppermute | solution.py:28
  739.2 57.8 %collective-permute-start.1 = (bf16[128,2048]{1,0:T(8,128)(2,1)S(1)}, bf16[128,2048]{1,0:T(8,128)(2,1)S(1)}, u32[]{:S(2)}, u32[]{:S(2)}) collective-permute-start(bf16[128,2048]{1,0:T(8,128)(2,1)S(1)} %convolution_convert_fusion.5), channel_id=1, source_target_pairs={{0,2},{1,3},{2,4},{3,5},{4,6},{5,7},{6,8},{7,9},{8,10},{9,11},{10,... | collective-permute-start | bytes 1572872 | tf_op jit(solution)/shard_map/while/body/eval_jaxpr/ppermute | solution.py:28
  741.2 62.9 %collective-permute-start.2 = (bf16[128,2048]{1,0:T(8,128)(2,1)S(1)}, bf16[128,2048]{1,0:T(8,128)(2,1)S(1)}, u32[]{:S(2)}, u32[]{:S(2)}) collective-permute-start(bf16[128,2048]{1,0:T(8,128)(2,1)S(1)} %convolution_convert_fusion.5), channel_id=1, source_target_pairs={{0,3},{1,4},{2,5},{3,6},{4,7},{5,8},{6,9},{7,10},{8,11},{9,12},{10... | collective-permute-start | bytes 1572872 | tf_op jit(solution)/shard_map/while/body/eval_jaxpr/ppermute | solution.py:28
  (18 other events, 152.9 us)
Sparse Core Ops, SparseCore 0:
  9.9 80.8 all-gather.1
where the time goes:
time: 843 us; the launch traced here: 831 us
  waiting for transfers between devices  490 us (58%)
  matrix products  97 us (12%)
  starting transfers between devices  89.7 us (11%)
  loops' own time  66.2 us (8%)
  local copies, waits for them, and re-layouts  42.2 us (5%)
  other arithmetic  17 us (2%)
  blocking collectives  14.7 us (2%)
  between operations  13.4 us (2%)
    ppermute x32, waiting for transfers between devices, from_behind(): return lax.ppermute(block, axis, route)  490 us
    ppermute x32, starting transfers between devices, from_behind(): return lax.ppermute(block, axis, route)  89.7 us
    another operation x1, loops' own time, entering(): return lax.fori_loop(0, place, one, state)  65.1 us
    dot_general x8, matrix products, tick(): jnp.dot(normed, keyval_full, preferred_element_type=jnp.float32)  38.6 us
    sub x8, matrix products, attend(): weights = jnp.exp(scores - row_top)  27.9 us
    dot_general x8, matrix products, attend(): jnp.einsum('hqk,khd->qhd', weights, value_part, preferred_element_type=jn...  18.2 us
  transfers between devices with their start and end apart: 33, of which 30 were waited for; matrix products, arithmetic and copies ran while one was open for 4% of the time, Pallas kernels for 0%

commit v1 on v0

v1 whole, which is shorter than its diff:
```python
import functools
import math

import jax
import jax.numpy as jnp
from jax import lax
from jax.experimental import pallas as pl
from jax.experimental.pallas import tpu as pltpu
from jax.sharding import PartitionSpec as P

MESH = pl.DeviceIdType.MESH
HEAD = 128
BLK = 128
RING = 4


def kernel(
    phases, chips, x_in, seg_in, wq_in, wkv_in, wo_in, out_ref,
    x_v, acc, wq_v, wkv_v, wo_v, wop_v, q_v, kv_v, bl_v, blo_v, bls_v, seg_v, bias_v,
    ssem, rsem, lsem, go_sem,
):
    width = x_v.shape[1]
    rows_dev = wkv_in.shape[0]
    rows_chip = 2 * rows_dev
    ph = lax.axis_index("phase")
    c = lax.axis_index("ctx")
    p = c // 2
    j = c % 2
    y = p // RING
    z = p % RING
    sib = c + 1 - 2 * j

    def at(phase, chip):
        return {"phase": phase, "ctx": chip * 2 + j}

    sibling = {"phase": ph, "ctx": sib}

    def chip_at(dy, dz):
        return ((y + dy + RING) % RING) * RING + (z + dz + RING) % RING

    y_next, y_prev = at(ph, chip_at(1, 0)), at(ph, chip_at(-1, 0))
    z_next, z_prev = at(ph, chip_at(0, 1)), at(ph, chip_at(0, -1))
    next1, next2 = at(ph, jnp.minimum(p + 1, chips - 1)), at(ph, jnp.minimum(p + 2, chips - 1))
    last1, last2 = at(ph, jnp.maximum(p - 1, 0)), at(ph, jnp.maximum(p - 2, 0))
    ph_next, ph_prev = at(jnp.minimum(ph + 1, phases - 1), p), at(jnp.maximum(ph - 1, 0), p)
    ph_over, ph_under = at(jnp.minimum(ph + RING, phases - 1), p), at(jnp.maximum(ph - RING, 0), p)
    has_next1, has_next2 = p + 1 < chips, p + 2 < chips
    has_last1, has_last2 = p >= 1, p >= 2
    is_first, is_last = ph == 0, ph == phases - 1
    has_over, has_under = ph + RING < phases, ph >= RING

    barrier = pltpu.get_barrier_semaphore()
    for device in (sibling, y_next, y_prev, z_next, z_prev):
        pl.semaphore_signal(barrier, inc=1, device_id=device, device_id_type=MESH)
    count = jnp.int32(5)
    for device, there in (
        (next1, has_next1), (next2, has_next2), (last1, has_last1), (last2, has_last2),
        (ph_next, ph + 1 < phases), (ph_prev, ph > 0), (ph_over, has_over), (ph_under, has_under),
    ):
        @pl.when(there)
        def _(device=device):
            pl.semaphore_signal(barrier, inc=1, device_id=device, device_id_type=MESH)

        count = count + there.astype(jnp.int32)
    pl.semaphore_wait(barrier, count)

    pending = []
    slots = iter(range(ssem.shape[0]))

    def copy(src, dst, slot, device):
        return pltpu.make_async_remote_copy(
            src_ref=src, dst_ref=dst, send_sem=ssem.at[slot], recv_sem=rsem.at[slot],
            device_id=device, device_id_type=MESH,
        )

    def send(src, dst, slot, device, when=None):
        made = copy(src, dst, slot, device)
        if when is None:
            made.start()
        else:
            pl.when(when)(made.start)
        pending.append((made, when))
        return made

    def recv(dst, slot):
        copy(dst, dst, slot, sibling).wait_recv()

    def run(when, body):
        pl.when(when)(body)

    local = []

    def load(src, dst):
        made = pltpu.make_async_copy(src, dst, lsem.at[len(local)])
        made.start()
        local.append(made)
        return made

    def columns(core, tile):
        start = core * 4 * HEAD + (tile // 2) * 2 * HEAD + (tile % 2) * 8 * HEAD
        return pl.ds(pl.multiple_of(start, 2 * HEAD), 2 * HEAD)

    own_rows = pl.ds(pl.multiple_of(c * rows_dev, rows_dev), rows_dev)
    shard_loads = [load(wkv_in.at[:, columns(j, t)], wkv_v.at[t, own_rows, :]) for t in range(4)]
    seg_load = load(seg_in, seg_v.at[3 + j])
    mine = pl.ds(pl.multiple_of(j * BLK, BLK), BLK)
    theirs = pl.ds(pl.multiple_of((1 - j) * BLK, BLK), BLK)
    wq_loads = [
        load(wq_in.at[:, pl.ds(pl.multiple_of(j * 4 * HEAD + t * 2 * HEAD, 2 * HEAD), 2 * HEAD)], wq_v.at[t])
        for t in range(2)
    ]
    wo_load = load(wo_in, wo_v)

    sib_rows = pl.ds(pl.multiple_of(sib * rows_dev, rows_dev), rows_dev)
    shard_slots = [next(slots) for _ in range(4)]
    seg_slots = [next(slots) for _ in range(3)]

    pl.when(has_under)(lambda: pl.semaphore_wait(go_sem, 1))
    for t in range(4):
        send(wkv_in.at[:, columns(1 - j, t)], wkv_v.at[t, own_rows, :], shard_slots[t], sibling)
    send(seg_in, seg_v.at[3 + j], seg_slots[0], sibling)

    wop_slots = [next(slots) for _ in range(4)]
    for k in range(4):
        send(wo_in.at[4 * j + k], wop_v.at[4 * j + k], wop_slots[k], ph_next, ph + 1 < phases)
    x_slot = next(slots)
    x_prev_slot = next(slots)
    x_load = pltpu.make_async_copy(x_in, x_v.at[mine], lsem.at[len(local)])
    x_direct = copy(x_in, x_v.at[mine], x_slot, sibling)

    @pl.when(ph < 2)
    def _():
        x_load.start()
        x_direct.start()

    for made in shard_loads:
        made.wait()
    for t in range(4):
        recv(wkv_v.at[t, sib_rows, :], shard_slots[t])

    def slab(chip, first, count_):
        return wkv_v.at[pl.ds(first, count_), pl.ds(pl.multiple_of(chip * rows_chip, rows_chip), rows_chip), :]

    sets = []
    for s in range(2):
        sets.append(dict(
            tile=2 * s,
            prim=(y_next, y_prev) if s == 0 else (z_next, z_prev),
            sec=(z_next, z_prev) if s == 0 else (y_next, y_prev),
            chip=(lambda a, b: chip_at(a, b)) if s == 0 else (lambda a, b: chip_at(b, a)),
            pslot=[next(slots) for _ in range(4)],
            sslot={dp: [next(slots) for _ in range(4)] for dp in (0, -1, 1, 2)},
        ))

    def ring_send(g, ring, slot, dp):
        piece = slab(g["chip"](dp, 0), g["tile"], 2)
        send(piece, piece, slot[0], ring[0])
        send(piece, piece, slot[1], ring[1])

    def ring_forward(g, ring, slot, before, after):
        piece = slab(before, g["tile"], 2)
        recv(piece, slot[0])
        half = slab(before, g["tile"], 1)
        send(half, half, slot[2], ring[0])
        piece = slab(after, g["tile"], 2)
        recv(piece, slot[1])
        half = slab(after, g["tile"] + 1, 1)
        send(half, half, slot[3], ring[1])

    def ring_end(g, slot, far):
        recv(slab(far, g["tile"], 1), slot[2])
        recv(slab(far, g["tile"] + 1, 1), slot[3])

    for g in sets:
        ring_send(g, g["prim"], g["pslot"], 0)
        ring_send(g, g["sec"], g["sslot"][0], 0)
    for g in sets:
        ring_forward(g, g["prim"], g["pslot"], g["chip"](-1, 0), g["chip"](1, 0))
        ring_send(g, g["sec"], g["sslot"][-1], -1)
        ring_send(g, g["sec"], g["sslot"][1], 1)
    for g in sets:
        ring_forward(g, g["sec"], g["sslot"][0], g["chip"](0, -1), g["chip"](0, 1))
    for g in sets:
        ring_end(g, g["pslot"], g["chip"](2, 0))
        ring_send(g, g["sec"], g["sslot"][2], 2)
    for dp in (-1, 1, 2):
        for g in sets:
            ring_forward(g, g["sec"], g["sslot"][dp], g["chip"](dp, -1), g["chip"](dp, 1))

    seg_load.wait()
    recv(seg_v.at[4 - j], seg_slots[0])
    send(seg_v.at[pl.ds(3, 2)], seg_v.at[pl.ds(1, 2)], seg_slots[1], next1, has_next1)
    send(seg_v.at[4], seg_v.at[0], seg_slots[2], next2, has_next2)

    @pl.when(jnp.logical_not(has_last1))
    def _():
        seg_v[1:3] = jnp.full((2,) + seg_v.shape[1:], -1.0, jnp.float32)
        kv_v[:, :, BLK:3 * BLK, :] = jnp.zeros((4, 2, 2 * BLK, HEAD), jnp.bfloat16)

    @pl.when(jnp.logical_not(has_last2))
    def _():
        seg_v[0] = jnp.full(seg_v.shape[1:], -1.0, jnp.float32)
        kv_v[:, :, 0:BLK, :] = jnp.zeros((4, 2, BLK, HEAD), jnp.bfloat16)

    run(has_last1, lambda: recv(seg_v.at[pl.ds(1, 2)], seg_slots[1]))
    run(has_last2, lambda: recv(seg_v.at[0], seg_slots[2]))

    row_id = lax.broadcasted_iota(jnp.int32, (BLK, BLK), 0)
    col_id = lax.broadcasted_iota(jnp.int32, (BLK, BLK), 1)
    causal = col_id <= row_id
    for i in range(2):
        asking = jnp.transpose(jnp.broadcast_to(seg_v[3 + i, 0:1, :], (BLK, BLK)))
        for b in range(4):
            asked = jnp.broadcast_to(seg_v[i + b, 0:1, :], (BLK, BLK))
            ok = asking == asked
            if b == 3:
                ok = ok & causal
            bias_v[i, :, b * BLK:(b + 1) * BLK] = jnp.where(ok, 0.0, -1e30).astype(jnp.float32)

    for dp in (0, -1, 1, 2):
        for g in sets:
            ring_end(g, g["sslot"][dp], g["chip"](dp, 2))
    for made in wq_loads:
        made.wait()
    wo_load.wait()

    @pl.when(has_over)
    def _():
        pl.semaphore_signal(go_sem, inc=1, device_id=ph_over, device_id_type=MESH)

    wop_relay = [next(slots) for _ in range(4)]
    relays = []
    for k in range(4):
        relays.append(copy(wop_v.at[4 * j + k], wop_v.at[4 * j + k], wop_relay[k], sibling))
    x_relay = copy(x_v.at[mine], x_v.at[mine], x_slot, sibling)

    @pl.when(ph > 0)
    def _():
        for k in range(4):
            recv(wop_v.at[4 * j + k], wop_slots[k])
            relays[k].start()

    @pl.when(ph < 2)
    def _():
        x_load.wait()
        x_direct.wait_send()

    @pl.when(ph >= 2)
    def _():
        recv(x_v.at[mine], x_prev_slot)
        x_relay.start()
        x_relay.wait_send()

    recv(x_v.at[theirs], x_slot)

    bl_slots = [next(slots) for _ in range(4)]
    bl_relay_slots = [next(slots) for _ in range(4)]
    bl_relays = [copy(bl_v.at[4 * j + h], bl_v.at[4 * j + h], bl_relay_slots[h], sibling) for h in range(4)]
    step = 512 if width % 512 == 0 else width

    @pl.when(ph > 0)
    def _():
        for k in range(4):
            recv(wop_v.at[4 * (1 - j) + k], wop_relay[k])
        for h in range(4):
            recv(bl_v.at[4 * j + h], bl_slots[h])
            bl_relays[h].start()
            recv(bl_v.at[4 * (1 - j) + h], bl_relay_slots[h])
            lhs = jnp.concatenate([bl_v[h], bl_v[4 + h]], axis=1)
            for n in range(0, width, step):
                rhs = jnp.concatenate([wop_v[h, :, n:n + step], wop_v[4 + h, :, n:n + step]], axis=0)
                part = jnp.dot(lhs, rhs, preferred_element_type=jnp.float32)
                if h == 0:
                    acc[:, n:n + step] = part
                elif h < 3:
                    acc[:, n:n + step] += part
                else:
                    total = x_v[:, n:n + step].astype(jnp.float32) + (acc[:, n:n + step] + part)
                    x_v[:, n:n + step] = total.astype(jnp.bfloat16)

    send(x_v.at[mine], x_v.at[mine], x_prev_slot, ph_next, (ph > 0) & (ph + 1 < phases))

    square = jnp.zeros((2 * BLK, 1), jnp.float32)
    for n in range(0, width, step):
        part = x_v[:, n:n + step].astype(jnp.float32)
        square = square + jnp.sum(part * part, axis=1, keepdims=True)
    scale_rows = lax.rsqrt(square * (1.0 / width) + 1e-05)

    halo_slots = [[next(slots), next(slots)] for _ in range(4)]
    stream = x_v[...]

    def project(weights):
        return (jnp.dot(stream, weights, preferred_element_type=jnp.float32) * scale_rows).astype(jnp.bfloat16)

    for t in range(2):
        for kind in range(2):
            made = project(wkv_v[2 * t + kind])
            kv_v[2 * t, kind, 3 * BLK:5 * BLK, :] = made[:, :HEAD]
            kv_v[2 * t + 1, kind, 3 * BLK:5 * BLK, :] = made[:, HEAD:]
        for h in (2 * t, 2 * t + 1):
            send(kv_v.at[h, :, pl.ds(3 * BLK, 2 * BLK), :], kv_v.at[h, :, pl.ds(BLK, 2 * BLK), :],
                 halo_slots[h][0], next1, has_next1)
            send(kv_v.at[h, :, pl.ds(4 * BLK, BLK), :], kv_v.at[h, :, pl.ds(0, BLK), :],
                 halo_slots[h][1], next2, has_next2)
    for t in range(2):
        made = project(wq_v[t])
        q_v[2 * t] = made[:, :HEAD]
        q_v[2 * t + 1] = made[:, HEAD:]

    bls_slots = [next(slots) for _ in range(4)]
    for h in range(4):
        run(has_last1, lambda h=h: recv(kv_v.at[h, :, pl.ds(BLK, 2 * BLK), :], halo_slots[h][0]))
        run(has_last2, lambda h=h: recv(kv_v.at[h, :, pl.ds(0, BLK), :], halo_slots[h][1]))
        for i in range(2):
            keys = kv_v[h, 0, i * BLK:(i + 4) * BLK, :]
            values = kv_v[h, 1, i * BLK:(i + 4) * BLK, :]
            scores = lax.dot_general(
                q_v[h, i * BLK:(i + 1) * BLK, :], keys, (((1,), (1,)), ((), ())),
                preferred_element_type=jnp.float32,
            )
            scores = scores * (1.0 / math.sqrt(HEAD)) + bias_v[i]
            top = jnp.max(scores, axis=1, keepdims=True)
            weights = jnp.exp(scores - top)
            total = jnp.sum(weights, axis=1, keepdims=True)
            mixed = jnp.dot(weights.astype(jnp.bfloat16), values, preferred_element_type=jnp.float32)
            blo_v[h, i * BLK:(i + 1) * BLK, :] = (mixed / total).astype(jnp.bfloat16)
        send(blo_v.at[h], bl_v.at[4 * j + h], bl_slots[h], ph_next, ph + 1 < phases)
        send(blo_v.at[h, theirs, :], bls_v.at[h], bls_slots[h], sibling)

    for h in range(4):
        recv(bls_v.at[h], bls_slots[h])
    own = jnp.concatenate([blo_v[h, mine, :] for h in range(4)], axis=1)
    other = jnp.concatenate([bls_v[h] for h in range(4)], axis=1)
    for n in range(0, width, step):
        first = wo_v[pl.ds(4 * j, 4), :, n:n + step].reshape(4 * HEAD, step)
        second = wo_v[pl.ds(4 * (1 - j), 4), :, n:n + step].reshape(4 * HEAD, step)
        update = jnp.dot(own, first, preferred_element_type=jnp.float32)
        update = update + jnp.dot(other, second, preferred_element_type=jnp.float32)
        out_ref[:, n:n + step] = (x_v[mine, n:n + step].astype(jnp.float32) + update).astype(jnp.bfloat16)

    for made, when in pending:
        if when is None:
            made.wait_send()
        else:
            pl.when(when)(made.wait_send)

    @pl.when(ph > 0)
    def _():
        for made in relays + bl_relays:
            made.wait_send()


def solution(mesh):
    phases, devices = mesh.shape["phase"], mesh.shape["ctx"]
    chips = devices // 2

    def local(inputs, segment_ids, w_query, w_keyval, w_out):
        width = inputs.shape[2]
        rows_dev = w_keyval.shape[1]
        seg = jnp.broadcast_to(segment_ids.astype(jnp.float32), (8, BLK))
        any_space = pl.BlockSpec(memory_space=pl.ANY)
        n_slots = 96
        made = pl.pallas_call(
            functools.partial(kernel, phases, chips),
            out_shape=jax.ShapeDtypeStruct((BLK, width), jnp.bfloat16),
            in_specs=[any_space] * 5,
            out_specs=pl.BlockSpec(memory_space=pltpu.VMEM),
            scratch_shapes=[
                pltpu.VMEM((2 * BLK, width), jnp.bfloat16),
                pltpu.VMEM((2 * BLK, width), jnp.float32),
                pltpu.VMEM((2, width, 2 * HEAD), jnp.bfloat16),
                pltpu.VMEM((4, width, 2 * HEAD), jnp.bfloat16),
                pltpu.VMEM((8, HEAD, width), jnp.bfloat16),
                pltpu.VMEM((8, HEAD, width), jnp.bfloat16),
                pltpu.VMEM((4, 2 * BLK, HEAD), jnp.bfloat16),
                pltpu.VMEM((4, 2, 5 * BLK, HEAD), jnp.bfloat16),
                pltpu.VMEM((8, 2 * BLK, HEAD), jnp.bfloat16),
                pltpu.VMEM((4, 2 * BLK, HEAD), jnp.bfloat16),
                pltpu.VMEM((4, BLK, HEAD), jnp.bfloat16),
                pltpu.VMEM((5, 8, BLK), jnp.float32),
                pltpu.VMEM((2, BLK, 4 * BLK), jnp.float32),
                pltpu.SemaphoreType.DMA((n_slots,)),
                pltpu.SemaphoreType.DMA((n_slots,)),
                pltpu.SemaphoreType.DMA((16,)),
                pltpu.SemaphoreType.REGULAR,
            ],
            compiler_params=pltpu.CompilerParams(
                collective_id=0, has_side_effects=True, vmem_limit_bytes=56 * 1024 * 1024
            ),
        )(
            inputs.reshape(BLK, width), seg, w_query.reshape(width, -1),
            w_keyval.reshape(rows_dev, -1), w_out.reshape(8, HEAD, width),
        )
        return made.reshape(1, 1, BLK, width)

    placed = (
        P(None, "ctx", None),
        P(None, "ctx"),
        P("phase", None, None),
        P("phase", "ctx", None),
        P("phase", None, None),
    )
    return jax.shard_map(
        local, mesh=mesh, in_specs=placed, out_specs=P("phase", None, "ctx", None), check_vma=False
    )
```

time: 843 us -> 265 us (0.31); the launches traced: 831 us -> 265 us
  waiting for transfers between devices: 490 us -> 0 us
  Pallas kernels: 0 us -> 262 us
  matrix products: 97 us -> 0 us
  starting transfers between devices: 89.7 us -> 0 us
  loops' own time: 66.2 us -> 0 us
  local copies, waits for them, and re-layouts: 42.2 us -> 2.48 us
  other arithmetic: 17 us -> 0.66 us
  blocking collectives: 14.7 us -> 0 us
  between operations: 13.4 us -> 0.01 us
    ppermute x32 -> x0, waiting for transfers between devices: 490 us -> none  [from_behind(): return lax.ppermute(block, axis, route)]
    pallas_call x0 -> x1, Pallas kernels: none -> 262 us  [local(): pl.pallas_call(functools.partial(kernel, phases, chips), out_shape=jax.Sh...]
    ppermute x32 -> x0, starting transfers between devices: 89.7 us -> none  [from_behind(): return lax.ppermute(block, axis, route)]
    dot_general x32 -> x0, matrix products: 69.1 us -> none  [the longest x8 38.6 us: tick(): jnp.dot(normed, keyval_full, preferred_element_type=jnp.float32)]
    another operation x2 -> x0, loops' own time: 66.2 us -> none  [the longest x1 65.1 us: entering(): return lax.fori_loop(0, place, one, state)]
    sub x8 -> x0, matrix products: 27.9 us -> none  [attend(): weights = jnp.exp(scores - row_top)]
    dynamic_slice x25 -> x0, local copies, waits for them, and re-layouts: 16.3 us -> none  [one(): lax.dynamic_index_in_dim(a, hop, 0, False)]
    unnamed x1 -> x0, blocking collectives: 14.7 us -> none
  transfers between devices with their start and end apart: 33 -> 0, of which waited for: 30 -> 0; matrix products, arithmetic and copies ran while one was open for 4% -> 0% of each run, Pallas kernels for 0% -> 0%
where the time goes in v1:
time: 265 us
  Pallas kernels  262 us (99%)
    pallas_call x1, Pallas kernels, local(): pl.pallas_call(functools.partial(kernel, phases, chips), out_shape=jax.Sh...  262 us

profile of v1, /device:TPU:63, one launch (start us, length us, event | category | flops | bytes accessed | tf_op | source)
XLA Modules:
  0.0 264.8 jit_solution(10144172109593670338)
XLA Ops:
  0.0 0.7 convert_bitcast_fusion
  0.7 0.6 broadcast_in_dim.8.seg_in
  1.3 261.7 %shard_map.55 = bf16[128,2048]{1,0:T(8,128)(2,1)} custom-call(bf16[128,2048]{1,0:T(8,128)(2,1)} %bitcast.10, f32[8,128]{1,0:T(8,128)} %broadcast_in_dim.8.seg_in, bf16[2048,1024]{1,0:T(8,128)(2,1)} %bitcast.7, bf16[64,2048]{1,0:T(8,128)(2,1)} %bitcast.11, bf16[8,128,2048]{2,1,0:T(8,128)(2,1)} %bitcast.8), custom_call_target="tpu_custom_call" | custom-call | tf_op jit(solution)/shard_map/pallas_call | solution.py:363
  262.9 1.9 copy.7

commit v2 on v1

--- a/solution.py
+++ b/solution.py
@@ -16,7 +16,7 @@
 
 def kernel(
     phases, chips, x_in, seg_in, wq_in, wkv_in, wo_in, out_ref,
-    x_v, acc, wq_v, wkv_v, wo_v, wop_v, q_v, kv_v, bl_v, blo_v, bls_v, seg_v, bias_v,
+    x_v, acc, wq_v, wkv_v, wo_v, wop_v, q_v, kv_v, bl_v, blo_v, bls_v, seg_v, bias_v, rel_v,
     ssem, rsem, lsem, go_sem,
 ):
     width = x_v.shape[1]
@@ -48,14 +48,22 @@
     has_last1, has_last2 = p >= 1, p >= 2
     is_first, is_last = ph == 0, ph == phases - 1
     has_over, has_under = ph + RING < phases, ph >= RING
+    late_helper = ph % RING < RING - 1
+    helper = jnp.where(ph % RING > 0, ph - 1, ph + RING - 1)
+    helped = jnp.where(late_helper, ph + 1, ph - RING + 1)
+    turn_out, turn_in = ph == RING - 1, ph == RING
 
     barrier = pltpu.get_barrier_semaphore()
-    for device in (sibling, y_next, y_prev, z_next, z_prev):
+    for device in (sibling, y_next, y_prev, z_next, z_prev, at(helper, p), at(helped, p)):
         pl.semaphore_signal(barrier, inc=1, device_id=device, device_id_type=MESH)
-    count = jnp.int32(5)
+    count = jnp.int32(7)
     for device, there in (
         (next1, has_next1), (next2, has_next2), (last1, has_last1), (last2, has_last2),
         (ph_next, ph + 1 < phases), (ph_prev, ph > 0), (ph_over, has_over), (ph_under, has_under),
+        (at(helped, jnp.minimum(p + 1, chips - 1)), has_next1), (at(helped, jnp.minimum(p + 2, chips - 1)), has_next2),
+        (at(helper, jnp.maximum(p - 1, 0)), has_last1), (at(helper, jnp.maximum(p - 2, 0)), has_last2),
+        (at(jnp.minimum(ph + 1, phases - 1), chip_at(0, -1)), turn_out),
+        (at(jnp.maximum(ph - 1, 0), chip_at(0, 1)), turn_in),
     ):
         @pl.when(there)
         def _(device=device):
@@ -115,14 +123,17 @@
     shard_slots = [next(slots) for _ in range(4)]
     seg_slots = [next(slots) for _ in range(3)]
 
-    pl.when(has_under)(lambda: pl.semaphore_wait(go_sem, 1))
     for t in range(4):
         send(wkv_in.at[:, columns(1 - j, t)], wkv_v.at[t, own_rows, :], shard_slots[t], sibling)
     send(seg_in, seg_v.at[3 + j], seg_slots[0], sibling)
 
     wop_slots = [next(slots) for _ in range(4)]
-    for k in range(4):
-        send(wo_in.at[4 * j + k], wop_v.at[4 * j + k], wop_slots[k], ph_next, ph + 1 < phases)
+
+    def send_wop(when, devices):
+        for k in range(4):
+            send(wo_in.at[4 * j + k], wop_v.at[4 * j + k], wop_slots[k], devices[k // 2], when)
+
+    send_wop(is_first, (ph_next, ph_next))
     x_slot = next(slots)
     x_prev_slot = next(slots)
     x_load = pltpu.make_async_copy(x_in, x_v.at[mine], lsem.at[len(local)])
@@ -171,6 +182,7 @@
         recv(slab(far, g["tile"], 1), slot[2])
         recv(slab(far, g["tile"] + 1, 1), slot[3])
 
+    pl.when(has_under)(lambda: pl.semaphore_wait(go_sem, 1))
     for g in sets:
         ring_send(g, g["prim"], g["pslot"], 0)
         ring_send(g, g["sec"], g["sslot"][0], 0)
@@ -224,9 +236,30 @@
         made.wait()
     wo_load.wait()
 
-    @pl.when(has_over)
-    def _():
-        pl.semaphore_signal(go_sem, inc=1, device_id=ph_over, device_id_type=MESH)
+    halo_slots = [[next(slots) for _ in range(4)] for _ in range(4)]
+    rel_slots = [next(slots) for _ in range(4)]
+    rel_copies = []
+    for h in range(4):
+        rel_copies.append((copy(rel_v.at[h], kv_v.at[h, 1, pl.ds(BLK, 2 * BLK), :], halo_slots[h][2],
+                                at(helped, jnp.minimum(p + 1, chips - 1))), has_next1))
+        rel_copies.append((copy(rel_v.at[h, pl.ds(BLK, BLK), :], kv_v.at[h, 1, pl.ds(0, BLK), :], halo_slots[h][3],
+                                at(helped, jnp.minimum(p + 2, chips - 1))), has_next2))
+
+    def help_halo():
+        @pl.when(has_next1)
+        def _():
+            for h in range(4):
+                recv(rel_v.at[h], rel_slots[h])
+                rel_copies[2 * h][0].start()
+                pl.when(has_next2)(rel_copies[2 * h + 1][0].start)
+
+        @pl.when(has_over)
+        def _():
+            pl.semaphore_signal(go_sem, inc=1, device_id=ph_over, device_id_type=MESH)
+
+    pl.when(jnp.logical_not(late_helper))(help_halo)
+    send_wop((ph > 0) & (ph + 1 < phases) & jnp.logical_not(turn_out), (ph_next, ph_next))
+    send_wop(turn_out, (ph_next, at(jnp.minimum(ph + 1, phases - 1), chip_at(0, -1))))
 
     wop_relay = [next(slots) for _ in range(4)]
     relays = []
@@ -286,7 +319,6 @@
         square = square + jnp.sum(part * part, axis=1, keepdims=True)
     scale_rows = lax.rsqrt(square * (1.0 / width) + 1e-05)
 
-    halo_slots = [[next(slots), next(slots)] for _ in range(4)]
     stream = x_v[...]
 
     def project(weights):
@@ -298,9 +330,10 @@
             kv_v[2 * t, kind, 3 * BLK:5 * BLK, :] = made[:, :HEAD]
             kv_v[2 * t + 1, kind, 3 * BLK:5 * BLK, :] = made[:, HEAD:]
         for h in (2 * t, 2 * t + 1):
-            send(kv_v.at[h, :, pl.ds(3 * BLK, 2 * BLK), :], kv_v.at[h, :, pl.ds(BLK, 2 * BLK), :],
+            send(kv_v.at[h, 1, pl.ds(3 * BLK, 2 * BLK), :], rel_v.at[h], rel_slots[h], at(helper, p), has_next1)
+            send(kv_v.at[h, 0, pl.ds(3 * BLK, 2 * BLK), :], kv_v.at[h, 0, pl.ds(BLK, 2 * BLK), :],
                  halo_slots[h][0], next1, has_next1)
-            send(kv_v.at[h, :, pl.ds(4 * BLK, BLK), :], kv_v.at[h, :, pl.ds(0, BLK), :],
+            send(kv_v.at[h, 0, pl.ds(4 * BLK, BLK), :], kv_v.at[h, 0, pl.ds(0, BLK), :],
                  halo_slots[h][1], next2, has_next2)
     for t in range(2):
         made = project(wq_v[t])
@@ -309,8 +342,9 @@
 
     bls_slots = [next(slots) for _ in range(4)]
     for h in range(4):
-        run(has_last1, lambda h=h: recv(kv_v.at[h, :, pl.ds(BLK, 2 * BLK), :], halo_slots[h][0]))
-        run(has_last2, lambda h=h: recv(kv_v.at[h, :, pl.ds(0, BLK), :], halo_slots[h][1]))
+        for kind in range(2):
+            run(has_last1, lambda h=h, kind=kind: recv(kv_v.at[h, kind, pl.ds(BLK, 2 * BLK), :], halo_slots[h][2 * kind]))
+            run(has_last2, lambda h=h, kind=kind: recv(kv_v.at[h, kind, pl.ds(0, BLK), :], halo_slots[h][2 * kind + 1]))
         for i in range(2):
             keys = kv_v[h, 0, i * BLK:(i + 4) * BLK, :]
             values = kv_v[h, 1, i * BLK:(i + 4) * BLK, :]
@@ -338,7 +372,8 @@
         update = update + jnp.dot(other, second, preferred_element_type=jnp.float32)
         out_ref[:, n:n + step] = (x_v[mine, n:n + step].astype(jnp.float32) + update).astype(jnp.bfloat16)
 
-    for made, when in pending:
+    pl.when(late_helper)(help_halo)
+    for made, when in pending + rel_copies:
         if when is None:
             made.wait_send()
         else:
@@ -359,7 +394,7 @@
         rows_dev = w_keyval.shape[1]
         seg = jnp.broadcast_to(segment_ids.astype(jnp.float32), (8, BLK))
         any_space = pl.BlockSpec(memory_space=pl.ANY)
-        n_slots = 96
+        n_slots = 128
         made = pl.pallas_call(
             functools.partial(kernel, phases, chips),
             out_shape=jax.ShapeDtypeStruct((BLK, width), jnp.bfloat16),
@@ -379,6 +414,7 @@
                 pltpu.VMEM((4, BLK, HEAD), jnp.bfloat16),
                 pltpu.VMEM((5, 8, BLK), jnp.float32),
                 pltpu.VMEM((2, BLK, 4 * BLK), jnp.float32),
+                pltpu.VMEM((4, 2 * BLK, HEAD), jnp.bfloat16),
                 pltpu.SemaphoreType.DMA((n_slots,)),
                 pltpu.SemaphoreType.DMA((n_slots,)),
                 pltpu.SemaphoreType.DMA((16,)),

time: 265 us -> 325 us (1.23)
  Pallas kernels: 262 us -> 322 us
    pallas_call x1, Pallas kernels: 262 us -> 322 us  [local(): pl.pallas_call(functools.partial(kernel, phases, chips), out_shape=jax.Sh...]
where the time goes in v2:
time: 325 us
  Pallas kernels  322 us (99%)
    pallas_call x1, Pallas kernels, local(): pl.pallas_call(functools.partial(kernel, phases, chips), out_shape=jax.Sh...  322 us

profile of v2, /device:TPU:63, one launch (start us, length us, event | category | flops | bytes accessed | tf_op | source)
XLA Modules:
  0.0 324.7 jit_solution(13605220173718711057)
XLA Ops:
  0.0 0.7 convert_bitcast_fusion
  0.7 0.6 broadcast_in_dim.8.seg_in
  1.3 321.6 %shard_map.55 = bf16[128,2048]{1,0:T(8,128)(2,1)} custom-call(bf16[128,2048]{1,0:T(8,128)(2,1)} %bitcast.10, f32[8,128]{1,0:T(8,128)} %broadcast_in_dim.8.seg_in, bf16[2048,1024]{1,0:T(8,128)(2,1)} %bitcast.7, bf16[64,2048]{1,0:T(8,128)(2,1)} %bitcast.11, bf16[8,128,2048]{2,1,0:T(8,128)(2,1)} %bitcast.8), custom_call_target="tpu_custom_call" | custom-call | tf_op jit(solution)/shard_map/pallas_call | solution.py:398
  322.8 1.9 copy.7

commit v3 on v2

--- a/solution.py
+++ b/solution.py
@@ -16,7 +16,7 @@
 
 def kernel(
     phases, chips, x_in, seg_in, wq_in, wkv_in, wo_in, out_ref,
-    x_v, acc, wq_v, wkv_v, wo_v, wop_v, q_v, kv_v, bl_v, blo_v, bls_v, seg_v, bias_v, rel_v,
+    x_v, acc, wq_v, wkv_v, wo_v, wop_v, q_v, kv_v, bl_v, blo_v, bls_v, seg_v, bias_v, rel_v, res_v, sq_v,
     ssem, rsem, lsem, go_sem,
 ):
     width = x_v.shape[1]
@@ -43,25 +43,44 @@
     next1, next2 = at(ph, jnp.minimum(p + 1, chips - 1)), at(ph, jnp.minimum(p + 2, chips - 1))
     last1, last2 = at(ph, jnp.maximum(p - 1, 0)), at(ph, jnp.maximum(p - 2, 0))
     ph_next, ph_prev = at(jnp.minimum(ph + 1, phases - 1), p), at(jnp.maximum(ph - 1, 0), p)
-    ph_over, ph_under = at(jnp.minimum(ph + RING, phases - 1), p), at(jnp.maximum(ph - RING, 0), p)
+    goer = jnp.where(ph < RING + 2, jnp.maximum(ph - RING + 1, 0), ph - RING)
     has_next1, has_next2 = p + 1 < chips, p + 2 < chips
     has_last1, has_last2 = p >= 1, p >= 2
     is_first, is_last = ph == 0, ph == phases - 1
-    has_over, has_under = ph + RING < phases, ph >= RING
-    late_helper = ph % RING < RING - 1
-    helper = jnp.where(ph % RING > 0, ph - 1, ph + RING - 1)
-    helped = jnp.where(late_helper, ph + 1, ph - RING + 1)
+    has_under = ph >= RING
+    goes_late, goes_early = (ph == 1) | (ph == 2), (ph == 2) | (ph == 3)
+    early_help, late_help = ph == 2 * RING - 1, (ph % RING < RING - 1)
+    has_helper, has_helped = ph > 0, ph != RING - 1
+    helper = jnp.where(ph == RING, 2 * RING - 1, jnp.maximum(ph - 1, 0))
+    helped = jnp.where(early_help, RING, jnp.minimum(ph + 1, phases - 1))
+    res_out, res_in = (ph >= 1) & (ph + 1 < phases), ph >= 2
+    early_pass, late_pass = ph >= RING + 2, ph < RING
+    has_pass = early_pass | late_pass
+    up = jnp.where(early_pass, 1, 0)
+
+    def passer(target):
+        low = target < RING
+        chip = jnp.where(low, chip_at(0, -1), p)
+        return at(jnp.where(low, target + RING, target - RING), chip)
+
+    pass_chip = chip_at(0, up)
+    pass_phase = jnp.where(early_pass, jnp.maximum(ph - RING, 0), jnp.minimum(ph + RING, phases - 1))
     turn_out, turn_in = ph == RING - 1, ph == RING
 
     barrier = pltpu.get_barrier_semaphore()
-    for device in (sibling, y_next, y_prev, z_next, z_prev, at(helper, p), at(helped, p)):
+    for device in (sibling, y_next, y_prev, z_next, z_prev):
         pl.semaphore_signal(barrier, inc=1, device_id=device, device_id_type=MESH)
-    count = jnp.int32(7)
+    count = jnp.int32(5)
     for device, there in (
         (next1, has_next1), (next2, has_next2), (last1, has_last1), (last2, has_last2),
-        (ph_next, ph + 1 < phases), (ph_prev, ph > 0), (ph_over, has_over), (ph_under, has_under),
-        (at(helped, jnp.minimum(p + 1, chips - 1)), has_next1), (at(helped, jnp.minimum(p + 2, chips - 1)), has_next2),
-        (at(helper, jnp.maximum(p - 1, 0)), has_last1), (at(helper, jnp.maximum(p - 2, 0)), has_last2),
+        (ph_next, ph + 1 < phases), (ph_prev, ph > 0), (at(goer, p), has_under), (at(ph + RING - 1, p), goes_late), (at(jnp.minimum(ph + RING, phases - 1), p), goes_early),
+        (at(helper, p), has_helper), (at(helped, p), has_helped),
+        (at(helped, jnp.minimum(p + 1, chips - 1)), has_helped & has_next1),
+        (at(helped, jnp.minimum(p + 2, chips - 1)), has_helped & has_next2),
+        (at(helper, jnp.maximum(p - 1, 0)), has_helper & has_last1),
+        (at(helper, jnp.maximum(p - 2, 0)), has_helper & has_last2),
+        (passer(jnp.minimum(ph + 1, phases - 1)), res_out), (passer(ph), res_in),
+        (at(jnp.maximum(pass_phase - 1, 0), pass_chip), has_pass), (at(pass_phase, pass_chip), has_pass),
         (at(jnp.minimum(ph + 1, phases - 1), chip_at(0, -1)), turn_out),
         (at(jnp.maximum(ph - 1, 0), chip_at(0, 1)), turn_in),
     ):
@@ -133,9 +152,11 @@
         for k in range(4):
             send(wo_in.at[4 * j + k], wop_v.at[4 * j + k], wop_slots[k], devices[k // 2], when)
 
-    send_wop(is_first, (ph_next, ph_next))
+    send_wop((ph + 1 < phases) & jnp.logical_not(turn_out), (ph_next, ph_next))
     x_slot = next(slots)
-    x_prev_slot = next(slots)
+    x_prev_slots = [next(slots) for _ in range(4)]
+    x_relay_slots = [next(slots) for _ in range(4)]
+    res_slots = [next(slots) for _ in range(4)]
     x_load = pltpu.make_async_copy(x_in, x_v.at[mine], lsem.at[len(local)])
     x_direct = copy(x_in, x_v.at[mine], x_slot, sibling)
 
@@ -182,10 +203,40 @@
         recv(slab(far, g["tile"], 1), slot[2])
         recv(slab(far, g["tile"] + 1, 1), slot[3])
 
+    seg_load.wait()
+    recv(seg_v.at[4 - j], seg_slots[0])
+    send(seg_v.at[pl.ds(3, 2)], seg_v.at[pl.ds(1, 2)], seg_slots[1], next1, has_next1)
+    send(seg_v.at[4], seg_v.at[0], seg_slots[2], next2, has_next2)
+
+    @pl.when(jnp.logical_not(has_last1))
+    def _():
+        seg_v[1:3] = jnp.full((2,) + seg_v.shape[1:], -1.0, jnp.float32)
+        kv_v[:, :, BLK:3 * BLK, :] = jnp.zeros((4, 2, 2 * BLK, HEAD), jnp.bfloat16)
+
+    @pl.when(jnp.logical_not(has_last2))
+    def _():
+        seg_v[0] = jnp.full(seg_v.shape[1:], -1.0, jnp.float32)
+        kv_v[:, :, 0:BLK, :] = jnp.zeros((4, 2, BLK, HEAD), jnp.bfloat16)
+
     pl.when(has_under)(lambda: pl.semaphore_wait(go_sem, 1))
     for g in sets:
         ring_send(g, g["prim"], g["pslot"], 0)
         ring_send(g, g["sec"], g["sslot"][0], 0)
+    run(has_last1, lambda: recv(seg_v.at[pl.ds(1, 2)], seg_slots[1]))
+    run(has_last2, lambda: recv(seg_v.at[0], seg_slots[2]))
+
+    row_id = lax.broadcasted_iota(jnp.int32, (BLK, BLK), 0)
+    col_id = lax.broadcasted_iota(jnp.int32, (BLK, BLK), 1)
+    causal = col_id <= row_id
+    for i in range(2):
+        asking = jnp.transpose(jnp.broadcast_to(seg_v[3 + i, 0:1, :], (BLK, BLK)))
+        for b in range(4):
+            asked = jnp.broadcast_to(seg_v[i + b, 0:1, :], (BLK, BLK))
+            ok = asking == asked
+            if b == 3:
+                ok = ok & causal
+            bias_v[i, :, b * BLK:(b + 1) * BLK] = jnp.where(ok, 0.0, -1e30).astype(jnp.float32)
+
     for g in sets:
         ring_forward(g, g["prim"], g["pslot"], g["chip"](-1, 0), g["chip"](1, 0))
         ring_send(g, g["sec"], g["sslot"][-1], -1)
@@ -199,36 +250,6 @@
         for g in sets:
             ring_forward(g, g["sec"], g["sslot"][dp], g["chip"](dp, -1), g["chip"](dp, 1))
 
-    seg_load.wait()
-    recv(seg_v.at[4 - j], seg_slots[0])
-    send(seg_v.at[pl.ds(3, 2)], seg_v.at[pl.ds(1, 2)], seg_slots[1], next1, has_next1)
-    send(seg_v.at[4], seg_v.at[0], seg_slots[2], next2, has_next2)
-
-    @pl.when(jnp.logical_not(has_last1))
-    def _():
-        seg_v[1:3] = jnp.full((2,) + seg_v.shape[1:], -1.0, jnp.float32)
-        kv_v[:, :, BLK:3 * BLK, :] = jnp.zeros((4, 2, 2 * BLK, HEAD), jnp.bfloat16)
-
-    @pl.when(jnp.logical_not(has_last2))
-    def _():
-        seg_v[0] = jnp.full(seg_v.shape[1:], -1.0, jnp.float32)
-        kv_v[:, :, 0:BLK, :] = jnp.zeros((4, 2, BLK, HEAD), jnp.bfloat16)
-
-    run(has_last1, lambda: recv(seg_v.at[pl.ds(1, 2)], seg_slots[1]))
-    run(has_last2, lambda: recv(seg_v.at[0], seg_slots[2]))
-
-    row_id = lax.broadcasted_iota(jnp.int32, (BLK, BLK), 0)
-    col_id = lax.broadcasted_iota(jnp.int32, (BLK, BLK), 1)
-    causal = col_id <= row_id
-    for i in range(2):
-        asking = jnp.transpose(jnp.broadcast_to(seg_v[3 + i, 0:1, :], (BLK, BLK)))
-        for b in range(4):
-            asked = jnp.broadcast_to(seg_v[i + b, 0:1, :], (BLK, BLK))
-            ok = asking == asked
-            if b == 3:
-                ok = ok & causal
-            bias_v[i, :, b * BLK:(b + 1) * BLK] = jnp.where(ok, 0.0, -1e30).astype(jnp.float32)
-
     for dp in (0, -1, 1, 2):
         for g in sets:
             ring_end(g, g["sslot"][dp], g["chip"](dp, 2))
@@ -241,9 +262,9 @@
     rel_copies = []
     for h in range(4):
         rel_copies.append((copy(rel_v.at[h], kv_v.at[h, 1, pl.ds(BLK, 2 * BLK), :], halo_slots[h][2],
-                                at(helped, jnp.minimum(p + 1, chips - 1))), has_next1))
+                                at(helped, jnp.minimum(p + 1, chips - 1))), has_helped & has_next1))
         rel_copies.append((copy(rel_v.at[h, pl.ds(BLK, BLK), :], kv_v.at[h, 1, pl.ds(0, BLK), :], halo_slots[h][3],
-                                at(helped, jnp.minimum(p + 2, chips - 1))), has_next2))
+                                at(helped, jnp.minimum(p + 2, chips - 1))), has_helped & has_next2))
 
     def help_halo():
         @pl.when(has_next1)
@@ -253,19 +274,41 @@
                 rel_copies[2 * h][0].start()
                 pl.when(has_next2)(rel_copies[2 * h + 1][0].start)
 
-        @pl.when(has_over)
+    def go(phase):
+        pl.semaphore_signal(go_sem, inc=1, device_id=at(jnp.minimum(phase, phases - 1), p), device_id_type=MESH)
+
+    piece = BLK // 4
+
+    def mine_at(k):
+        return x_v.at[pl.ds(pl.multiple_of(j * BLK + k * piece, piece), piece), :]
+
+    def theirs_at(k):
+        return x_v.at[pl.ds(pl.multiple_of((1 - j) * BLK + k * piece, piece), piece), :]
+
+    res_copies = [copy(res_v.at[k], mine_at(k), x_prev_slots[k], at(pass_phase, pass_chip)) for k in range(4)]
+    pass_all = ph == 0
+
+    def pass_residual():
+        @pl.when(pass_all)
         def _():
-            pl.semaphore_signal(go_sem, inc=1, device_id=ph_over, device_id_type=MESH)
-
-    pl.when(jnp.logical_not(late_helper))(help_halo)
-    send_wop((ph > 0) & (ph + 1 < phases) & jnp.logical_not(turn_out), (ph_next, ph_next))
+            for k in range(2):
+                recv(res_v.at[k], res_slots[k])
+                res_copies[k].start()
+
+        for k in range(2, 4):
+            recv(res_v.at[k], res_slots[k])
+            res_copies[k].start()
+
+    pl.when(goes_early)(lambda: go(ph + RING))
+    pl.when(early_pass)(pass_residual)
+    pl.when(early_help)(help_halo)
     send_wop(turn_out, (ph_next, at(jnp.minimum(ph + 1, phases - 1), chip_at(0, -1))))
 
     wop_relay = [next(slots) for _ in range(4)]
     relays = []
     for k in range(4):
         relays.append(copy(wop_v.at[4 * j + k], wop_v.at[4 * j + k], wop_relay[k], sibling))
-    x_relay = copy(x_v.at[mine], x_v.at[mine], x_slot, sibling)
+    x_relays = [copy(mine_at(k), mine_at(k), x_relay_slots[k], sibling) for k in range(4)]
 
     @pl.when(ph > 0)
     def _():
@@ -277,46 +320,69 @@
     def _():
         x_load.wait()
         x_direct.wait_send()
-
-    @pl.when(ph >= 2)
-    def _():
-        recv(x_v.at[mine], x_prev_slot)
-        x_relay.start()
-        x_relay.wait_send()
-
-    recv(x_v.at[theirs], x_slot)
+        recv(x_v.at[theirs], x_slot)
 
     bl_slots = [next(slots) for _ in range(4)]
     bl_relay_slots = [next(slots) for _ in range(4)]
     bl_relays = [copy(bl_v.at[4 * j + h], bl_v.at[4 * j + h], bl_relay_slots[h], sibling) for h in range(4)]
     step = 512 if width % 512 == 0 else width
 
+    def add_squares(n, rounded):
+        wide = rounded.astype(jnp.float32)
+        wide = wide * wide
+        lanes = wide[:, :HEAD]
+        for m in range(HEAD, step, HEAD):
+            lanes = lanes + wide[:, m:m + HEAD]
+        sq_v[...] = lanes if n == 0 else sq_v[...] + lanes
+
+
     @pl.when(ph > 0)
     def _():
         for k in range(4):
             recv(wop_v.at[4 * (1 - j) + k], wop_relay[k])
-        for h in range(4):
-            recv(bl_v.at[4 * j + h], bl_slots[h])
-            bl_relays[h].start()
-            recv(bl_v.at[4 * (1 - j) + h], bl_relay_slots[h])
-            lhs = jnp.concatenate([bl_v[h], bl_v[4 + h]], axis=1)
+        mine_head, their_head = 4 * j, 4 * (1 - j)
+        for h in range(5):
+            if h < 4:
+                recv(bl_v.at[mine_head + h], bl_slots[h])
+                bl_relays[h].start()
+            if h == 2:
+                @pl.when(ph >= 2)
+                def _():
+                    for k in range(4):
+                        recv(mine_at(k), x_prev_slots[k])
+                        x_relays[k].start()
+
+            if h == 4:
+                @pl.when(ph >= 2)
+                def _():
+                    for k in range(4):
+                        recv(theirs_at(k), x_relay_slots[k])
+                    for k in range(4):
+                        x_relays[k].wait_send()
+
+            if h > 0:
+                recv(bl_v.at[their_head + h - 1], bl_relay_slots[h - 1])
+            heads = ([mine_head + h] if h < 4 else []) + ([their_head + h - 1] if h > 0 else [])
+            lhs = jnp.concatenate([bl_v[head] for head in heads], axis=1)
             for n in range(0, width, step):
-                rhs = jnp.concatenate([wop_v[h, :, n:n + step], wop_v[4 + h, :, n:n + step]], axis=0)
+                rhs = jnp.concatenate([wop_v[head, :, n:n + step] for head in heads], axis=0)
                 part = jnp.dot(lhs, rhs, preferred_element_type=jnp.float32)
                 if h == 0:
                     acc[:, n:n + step] = part
-                elif h < 3:
+                elif h < 4:
                     acc[:, n:n + step] += part
                 else:
                     total = x_v[:, n:n + step].astype(jnp.float32) + (acc[:, n:n + step] + part)
-                    x_v[:, n:n + step] = total.astype(jnp.bfloat16)
-
-    send(x_v.at[mine], x_v.at[mine], x_prev_slot, ph_next, (ph > 0) & (ph + 1 < phases))
-
-    square = jnp.zeros((2 * BLK, 1), jnp.float32)
-    for n in range(0, width, step):
-        part = x_v[:, n:n + step].astype(jnp.float32)
-        square = square + jnp.sum(part * part, axis=1, keepdims=True)
+                    total = total.astype(jnp.bfloat16)
+                    x_v[:, n:n + step] = total
+                    add_squares(n, total)
+
+    @pl.when(is_first)
+    def _():
+        for n in range(0, width, step):
+            add_squares(n, x_v[:, n:n + step])
+
+    square = jnp.sum(sq_v[...], axis=1, keepdims=True)
     scale_rows = lax.rsqrt(square * (1.0 / width) + 1e-05)
 
     stream = x_v[...]
@@ -330,7 +396,11 @@
             kv_v[2 * t, kind, 3 * BLK:5 * BLK, :] = made[:, :HEAD]
             kv_v[2 * t + 1, kind, 3 * BLK:5 * BLK, :] = made[:, HEAD:]
         for h in (2 * t, 2 * t + 1):
-            send(kv_v.at[h, 1, pl.ds(3 * BLK, 2 * BLK), :], rel_v.at[h], rel_slots[h], at(helper, p), has_next1)
+            send(kv_v.at[h, 1, pl.ds(3 * BLK, 2 * BLK), :], rel_v.at[h], rel_slots[h], at(helper, p), has_helper & has_next1)
+            send(kv_v.at[h, 1, pl.ds(3 * BLK, 2 * BLK), :], kv_v.at[h, 1, pl.ds(BLK, 2 * BLK), :],
+                 halo_slots[h][2], next1, is_first & has_next1)
+            send(kv_v.at[h, 1, pl.ds(4 * BLK, BLK), :], kv_v.at[h, 1, pl.ds(0, BLK), :],
+                 halo_slots[h][3], next2, is_first & has_next2)
             send(kv_v.at[h, 0, pl.ds(3 * BLK, 2 * BLK), :], kv_v.at[h, 0, pl.ds(BLK, 2 * BLK), :],
                  halo_slots[h][0], next1, has_next1)
             send(kv_v.at[h, 0, pl.ds(4 * BLK, BLK), :], kv_v.at[h, 0, pl.ds(0, BLK), :],
@@ -339,6 +409,14 @@
         made = project(wq_v[t])
         q_v[2 * t] = made[:, :HEAD]
         q_v[2 * t + 1] = made[:, HEAD:]
+
+    for k in range(4):
+        if k < 2:
+            direct, around = res_out & jnp.logical_not(turn_out), turn_out
+            send(mine_at(k), mine_at(k), x_prev_slots[k], ph_next, direct)
+        else:
+            around = res_out
+        send(mine_at(k), res_v.at[k], res_slots[k], passer(jnp.minimum(ph + 1, phases - 1)), around)
 
     bls_slots = [next(slots) for _ in range(4)]
     for h in range(4):
@@ -361,6 +439,8 @@
         send(blo_v.at[h], bl_v.at[4 * j + h], bl_slots[h], ph_next, ph + 1 < phases)
         send(blo_v.at[h, theirs, :], bls_v.at[h], bls_slots[h], sibling)
 
+    pl.when(goes_late)(lambda: go(ph + RING - 1))
+
     for h in range(4):
         recv(bls_v.at[h], bls_slots[h])
     own = jnp.concatenate([blo_v[h, mine, :] for h in range(4)], axis=1)
@@ -372,8 +452,9 @@
         update = update + jnp.dot(other, second, preferred_element_type=jnp.float32)
         out_ref[:, n:n + step] = (x_v[mine, n:n + step].astype(jnp.float32) + update).astype(jnp.bfloat16)
 
-    pl.when(late_helper)(help_halo)
-    for made, when in pending + rel_copies:
+    pl.when(late_help)(help_halo)
+    pl.when(late_pass)(pass_residual)
+    for made, when in pending + rel_copies + [(made, has_pass if k > 1 else pass_all) for k, made in enumerate(res_copies)]:
         if when is None:
             made.wait_send()
         else:
@@ -415,6 +496,8 @@
                 pltpu.VMEM((5, 8, BLK), jnp.float32),
                 pltpu.VMEM((2, BLK, 4 * BLK), jnp.float32),
                 pltpu.VMEM((4, 2 * BLK, HEAD), jnp.bfloat16),
+                pltpu.VMEM((4, BLK // 4, width), jnp.bfloat16),
+                pltpu.VMEM((2 * BLK, HEAD), jnp.float32),
                 pltpu.SemaphoreType.DMA((n_slots,)),
                 pltpu.SemaphoreType.DMA((n_slots,)),
                 pltpu.SemaphoreType.DMA((16,)),

time: 325 us -> 246 us (0.76)
  Pallas kernels: 322 us -> 240 us
    pallas_call x1, Pallas kernels: 322 us -> 240 us  [local(): pl.pallas_call(functools.partial(kernel, phases, chips), out_shape=jax.Sh...]
where the time goes in v3:
time: 246 us; the launch traced here: 243 us
  Pallas kernels  240 us (98%)
  local copies, waits for them, and re-layouts  2.48 us (1%)
    pallas_call x1, Pallas kernels, local(): pl.pallas_call(functools.partial(kernel, phases, chips), out_shape=jax.Sh...  240 us

profile of v3, /device:TPU:63, one launch (start us, length us, event | category | flops | bytes accessed | tf_op | source)
XLA Modules:
  0.0 243.2 jit_solution(2942624209262445624)
XLA Ops:
  0.0 0.7 convert_bitcast_fusion
  0.7 0.6 broadcast_in_dim.8.seg_in
  1.3 240.1 %shard_map.55 = bf16[128,2048]{1,0:T(8,128)(2,1)} custom-call(bf16[128,2048]{1,0:T(8,128)(2,1)} %bitcast.10, f32[8,128]{1,0:T(8,128)} %broadcast_in_dim.8.seg_in, bf16[2048,1024]{1,0:T(8,128)(2,1)} %bitcast.7, bf16[64,2048]{1,0:T(8,128)(2,1)} %bitcast.11, bf16[8,128,2048]{2,1,0:T(8,128)(2,1)} %bitcast.8), custom_call_target="tpu_custom_call" | custom-call | tf_op jit(solution)/shard_map/pallas_call | solution.py:479
  241.3 1.9 copy.7

commit v4 on v3

--- a/solution.py
+++ b/solution.py
@@ -16,7 +16,7 @@
 
 def kernel(
     phases, chips, x_in, seg_in, wq_in, wkv_in, wo_in, out_ref,
-    x_v, acc, wq_v, wkv_v, wo_v, wop_v, q_v, kv_v, bl_v, blo_v, bls_v, seg_v, bias_v, rel_v, res_v, sq_v,
+    x_v, acc, wq_v, wkv_v, wo_v, wop_v, q_v, kv_v, bl_v, blo_v, bls_v, seg_v, bias_v, rel_v, far_v, res_v, sq_v, mix_v, top_v, sum_v,
     ssem, rsem, lsem, go_sem,
 ):
     width = x_v.shape[1]
@@ -54,17 +54,14 @@
     helper = jnp.where(ph == RING, 2 * RING - 1, jnp.maximum(ph - 1, 0))
     helped = jnp.where(early_help, RING, jnp.minimum(ph + 1, phases - 1))
     res_out, res_in = (ph >= 1) & (ph + 1 < phases), ph >= 2
-    early_pass, late_pass = ph >= RING + 2, ph < RING
-    has_pass = early_pass | late_pass
-    up = jnp.where(early_pass, 1, 0)
-
-    def passer(target):
-        low = target < RING
-        chip = jnp.where(low, chip_at(0, -1), p)
-        return at(jnp.where(low, target + RING, target - RING), chip)
-
-    pass_chip = chip_at(0, up)
-    pass_phase = jnp.where(early_pass, jnp.maximum(ph - RING, 0), jnp.minimum(ph + RING, phases - 1))
+    turn_pass = ph == 0
+    low, high = ph < RING, ph >= RING
+    far_chip = at(jnp.minimum(ph + RING, phases - 1), chip_at(0, -1))
+    far_from, far_phase = chip_at(0, 1), jnp.maximum(ph - RING, 0)
+    far_to = jnp.minimum(far_from + 2, chips - 1)
+    does_far = high & (far_from + 2 < chips)
+    two_back = jnp.maximum(p - 2, 0)
+    far_back = at(jnp.minimum(ph + RING, phases - 1), (two_back // RING) * RING + (two_back + RING - 1) % RING)
     turn_out, turn_in = ph == RING - 1, ph == RING
 
     barrier = pltpu.get_barrier_semaphore()
@@ -74,13 +71,14 @@
     for device, there in (
         (next1, has_next1), (next2, has_next2), (last1, has_last1), (last2, has_last2),
         (ph_next, ph + 1 < phases), (ph_prev, ph > 0), (at(goer, p), has_under), (at(ph + RING - 1, p), goes_late), (at(jnp.minimum(ph + RING, phases - 1), p), goes_early),
+        (far_chip, low & has_next2), (far_back, low & has_last2),
+        (at(far_phase, far_from), does_far), (at(far_phase, far_to), does_far),
         (at(helper, p), has_helper), (at(helped, p), has_helped),
         (at(helped, jnp.minimum(p + 1, chips - 1)), has_helped & has_next1),
         (at(helped, jnp.minimum(p + 2, chips - 1)), has_helped & has_next2),
         (at(helper, jnp.maximum(p - 1, 0)), has_helper & has_last1),
         (at(helper, jnp.maximum(p - 2, 0)), has_helper & has_last2),
-        (passer(jnp.minimum(ph + 1, phases - 1)), res_out), (passer(ph), res_in),
-        (at(jnp.maximum(pass_phase - 1, 0), pass_chip), has_pass), (at(pass_phase, pass_chip), has_pass),
+        (at(0, p), turn_out | turn_in), (at(RING - 1, p), turn_pass), (at(RING, p), turn_pass),
         (at(jnp.minimum(ph + 1, phases - 1), chip_at(0, -1)), turn_out),
         (at(jnp.maximum(ph - 1, 0), chip_at(0, 1)), turn_in),
     ):
@@ -138,6 +136,38 @@
     ]
     wo_load = load(wo_in, wo_v)
 
+    halo_slots = [[next(slots) for _ in range(4)] for _ in range(4)]
+    rel_slots = [next(slots) for _ in range(4)]
+    far_slots = [next(slots) for _ in range(4)]
+    helped_high = helped >= RING
+    rel_copies = []
+    for h in range(4):
+        rel_copies.append((copy(rel_v.at[h], kv_v.at[h, 1, pl.ds(BLK, 2 * BLK), :], halo_slots[h][2],
+                                at(helped, jnp.minimum(p + 1, chips - 1))),
+                           has_helped & has_next1 & (True if h > 0 else jnp.logical_not(helped_high))))
+    for h in range(1, 4):
+        rel_copies.append((copy(rel_v.at[h, pl.ds(BLK, BLK), :], kv_v.at[h, 1, pl.ds(0, BLK), :], halo_slots[h][3],
+                                at(helped, jnp.minimum(p + 2, chips - 1))), has_helped & has_next2 & helped_high))
+    far_copies = [
+        (copy(far_v.at[h], kv_v.at[h, 1, pl.ds(0, BLK), :], halo_slots[h][3], at(far_phase, far_to)), does_far)
+        for h in range(4)
+    ]
+
+    def help_halo():
+        for h in range(4):
+            @pl.when(rel_copies[h][1])
+            def _(h=h):
+                recv(rel_v.at[h], rel_slots[h])
+                rel_copies[h][0].start()
+
+            if h > 0:
+                pl.when(rel_copies[h + 3][1])(rel_copies[h + 3][0].start)
+
+    def help_far():
+        for h in range(4):
+            recv(far_v.at[h], far_slots[h])
+            far_copies[h][0].start()
+
     sib_rows = pl.ds(pl.multiple_of(sib * rows_dev, rows_dev), rows_dev)
     shard_slots = [next(slots) for _ in range(4)]
     seg_slots = [next(slots) for _ in range(3)]
@@ -218,6 +248,7 @@
         seg_v[0] = jnp.full(seg_v.shape[1:], -1.0, jnp.float32)
         kv_v[:, :, 0:BLK, :] = jnp.zeros((4, 2, BLK, HEAD), jnp.bfloat16)
 
+    pl.when(does_far & (ph < RING + 2))(help_far)
     pl.when(has_under)(lambda: pl.semaphore_wait(go_sem, 1))
     for g in sets:
         ring_send(g, g["prim"], g["pslot"], 0)
@@ -257,23 +288,6 @@
         made.wait()
     wo_load.wait()
 
-    halo_slots = [[next(slots) for _ in range(4)] for _ in range(4)]
-    rel_slots = [next(slots) for _ in range(4)]
-    rel_copies = []
-    for h in range(4):
-        rel_copies.append((copy(rel_v.at[h], kv_v.at[h, 1, pl.ds(BLK, 2 * BLK), :], halo_slots[h][2],
-                                at(helped, jnp.minimum(p + 1, chips - 1))), has_helped & has_next1))
-        rel_copies.append((copy(rel_v.at[h, pl.ds(BLK, BLK), :], kv_v.at[h, 1, pl.ds(0, BLK), :], halo_slots[h][3],
-                                at(helped, jnp.minimum(p + 2, chips - 1))), has_helped & has_next2))
-
-    def help_halo():
-        @pl.when(has_next1)
-        def _():
-            for h in range(4):
-                recv(rel_v.at[h], rel_slots[h])
-                rel_copies[2 * h][0].start()
-                pl.when(has_next2)(rel_copies[2 * h + 1][0].start)
-
     def go(phase):
         pl.semaphore_signal(go_sem, inc=1, device_id=at(jnp.minimum(phase, phases - 1), p), device_id_type=MESH)
 
@@ -285,22 +299,15 @@
     def theirs_at(k):
         return x_v.at[pl.ds(pl.multiple_of((1 - j) * BLK + k * piece, piece), piece), :]
 
-    res_copies = [copy(res_v.at[k], mine_at(k), x_prev_slots[k], at(pass_phase, pass_chip)) for k in range(4)]
-    pass_all = ph == 0
+    res_copies = [copy(res_v.at[k], mine_at(k), x_prev_slots[k], at(RING, p)) for k in range(1, 4)]
 
     def pass_residual():
-        @pl.when(pass_all)
-        def _():
-            for k in range(2):
-                recv(res_v.at[k], res_slots[k])
-                res_copies[k].start()
-
-        for k in range(2, 4):
+        for k in range(1, 4):
             recv(res_v.at[k], res_slots[k])
-            res_copies[k].start()
+            res_copies[k - 1].start()
 
     pl.when(goes_early)(lambda: go(ph + RING))
-    pl.when(early_pass)(pass_residual)
+    pl.when(does_far & (ph >= RING + 2))(help_far)
     pl.when(early_help)(help_halo)
     send_wop(turn_out, (ph_next, at(jnp.minimum(ph + 1, phases - 1), chip_at(0, -1))))
 
@@ -341,42 +348,50 @@
         for k in range(4):
             recv(wop_v.at[4 * (1 - j) + k], wop_relay[k])
         mine_head, their_head = 4 * j, 4 * (1 - j)
-        for h in range(5):
-            if h < 4:
-                recv(bl_v.at[mine_head + h], bl_slots[h])
-                bl_relays[h].start()
-            if h == 2:
-                @pl.when(ph >= 2)
-                def _():
-                    for k in range(4):
-                        recv(mine_at(k), x_prev_slots[k])
-                        x_relays[k].start()
-
-            if h == 4:
-                @pl.when(ph >= 2)
-                def _():
-                    for k in range(4):
-                        recv(theirs_at(k), x_relay_slots[k])
-                    for k in range(4):
-                        x_relays[k].wait_send()
-
-            if h > 0:
-                recv(bl_v.at[their_head + h - 1], bl_relay_slots[h - 1])
-            heads = ([mine_head + h] if h < 4 else []) + ([their_head + h - 1] if h > 0 else [])
+        def take(h):
+            recv(bl_v.at[mine_head + h], bl_slots[h])
+            bl_relays[h].start()
+
+        def project_heads(first):
+            heads = [mine_head + first, mine_head + first + 1, their_head + first, their_head + first + 1]
             lhs = jnp.concatenate([bl_v[head] for head in heads], axis=1)
             for n in range(0, width, step):
                 rhs = jnp.concatenate([wop_v[head, :, n:n + step] for head in heads], axis=0)
                 part = jnp.dot(lhs, rhs, preferred_element_type=jnp.float32)
-                if h == 0:
+                if first == 0:
                     acc[:, n:n + step] = part
-                elif h < 4:
-                    acc[:, n:n + step] += part
                 else:
                     total = x_v[:, n:n + step].astype(jnp.float32) + (acc[:, n:n + step] + part)
                     total = total.astype(jnp.bfloat16)
                     x_v[:, n:n + step] = total
                     add_squares(n, total)
 
+        take(0)
+        take(1)
+
+        @pl.when(ph >= 2)
+        def _():
+            for k in range(4):
+                recv(mine_at(k), x_prev_slots[k])
+                x_relays[k].start()
+
+        recv(bl_v.at[their_head], bl_relay_slots[0])
+        recv(bl_v.at[their_head + 1], bl_relay_slots[1])
+        take(2)
+        project_heads(0)
+        take(3)
+        recv(bl_v.at[their_head + 2], bl_relay_slots[2])
+        recv(bl_v.at[their_head + 3], bl_relay_slots[3])
+
+        @pl.when(ph >= 2)
+        def _():
+            for k in range(4):
+                recv(theirs_at(k), x_relay_slots[k])
+            for k in range(4):
+                x_relays[k].wait_send()
+
+        project_heads(2)
+
     @pl.when(is_first)
     def _():
         for n in range(0, width, step):
@@ -385,57 +400,85 @@
     square = jnp.sum(sq_v[...], axis=1, keepdims=True)
     scale_rows = lax.rsqrt(square * (1.0 / width) + 1e-05)
 
+    for k in range(4):
+        send(mine_at(k), mine_at(k), x_prev_slots[k], ph_next, res_out if k == 0 else res_out & jnp.logical_not(turn_out))
+        if k > 0:
+            send(mine_at(k), res_v.at[k], res_slots[k], at(0, p), turn_out)
     stream = x_v[...]
 
     def project(weights):
         return (jnp.dot(stream, weights, preferred_element_type=jnp.float32) * scale_rows).astype(jnp.bfloat16)
 
-    for t in range(2):
-        for kind in range(2):
+    for kind in (1, 0):
+        for t in range(2):
             made = project(wkv_v[2 * t + kind])
             kv_v[2 * t, kind, 3 * BLK:5 * BLK, :] = made[:, :HEAD]
             kv_v[2 * t + 1, kind, 3 * BLK:5 * BLK, :] = made[:, HEAD:]
-        for h in (2 * t, 2 * t + 1):
-            send(kv_v.at[h, 1, pl.ds(3 * BLK, 2 * BLK), :], rel_v.at[h], rel_slots[h], at(helper, p), has_helper & has_next1)
-            send(kv_v.at[h, 1, pl.ds(3 * BLK, 2 * BLK), :], kv_v.at[h, 1, pl.ds(BLK, 2 * BLK), :],
-                 halo_slots[h][2], next1, is_first & has_next1)
-            send(kv_v.at[h, 1, pl.ds(4 * BLK, BLK), :], kv_v.at[h, 1, pl.ds(0, BLK), :],
-                 halo_slots[h][3], next2, is_first & has_next2)
-            send(kv_v.at[h, 0, pl.ds(3 * BLK, 2 * BLK), :], kv_v.at[h, 0, pl.ds(BLK, 2 * BLK), :],
-                 halo_slots[h][0], next1, has_next1)
-            send(kv_v.at[h, 0, pl.ds(4 * BLK, BLK), :], kv_v.at[h, 0, pl.ds(0, BLK), :],
-                 halo_slots[h][1], next2, has_next2)
+            for h in (2 * t, 2 * t + 1):
+                both = kv_v.at[h, kind, pl.ds(3 * BLK, 2 * BLK), :]
+                odd = kv_v.at[h, kind, pl.ds(4 * BLK, BLK), :]
+                to_next1, to_next2 = kv_v.at[h, kind, pl.ds(BLK, 2 * BLK), :], kv_v.at[h, kind, pl.ds(0, BLK), :]
+                if kind == 0:
+                    send(both, to_next1, halo_slots[h][0], next1, has_next1)
+                    send(odd, to_next2, halo_slots[h][1], next2, has_next2 & high)
+                    continue
+                straight = is_first | high if h < 1 else is_first
+                send(both, rel_v.at[h], rel_slots[h], at(helper, p), has_next1 & jnp.logical_not(straight))
+                send(both, to_next1, halo_slots[h][2], next1, straight & has_next1)
+                if h < 1:
+                    send(odd, to_next2, halo_slots[h][3], next2, has_next2 & high)
+                send(odd, far_v.at[h], far_slots[h], far_chip, has_next2 & low)
     for t in range(2):
         made = project(wq_v[t])
         q_v[2 * t] = made[:, :HEAD]
         q_v[2 * t + 1] = made[:, HEAD:]
 
-    for k in range(4):
-        if k < 2:
-            direct, around = res_out & jnp.logical_not(turn_out), turn_out
-            send(mine_at(k), mine_at(k), x_prev_slots[k], ph_next, direct)
-        else:
-            around = res_out
-        send(mine_at(k), res_v.at[k], res_slots[k], passer(jnp.minimum(ph + 1, phases - 1)), around)
-
     bls_slots = [next(slots) for _ in range(4)]
+    factor = math.log2(math.e) / math.sqrt(HEAD)
+
+    def scored(h, i, keys, first):
+        query = q_v[h, i * BLK:(i + 1) * BLK, :]
+        scores = lax.dot_general(query, keys, (((1,), (1,)), ((), ())), preferred_element_type=jnp.float32)
+        return scores * factor + bias_v[i, :, first:first + keys.shape[0]]
+
+    def mix(weights, values):
+        return jnp.dot(weights.astype(jnp.bfloat16), values, preferred_element_type=jnp.float32)
+
+    near = ((0, 3 * BLK, 4 * BLK, 3 * BLK), (1, 3 * BLK, 5 * BLK, 2 * BLK))
+    far = ((0, 0, 3 * BLK, 0), (1, BLK, 3 * BLK, 0))
     for h in range(4):
+        scores = [scored(h, i, kv_v[h, 0, lo:hi, :], first) for i, lo, hi, first in near]
+        tops = [jnp.max(part, axis=1, keepdims=True) for part in scores]
+        weights = [jnp.exp2(part - top) for part, top in zip(scores, tops)]
+        sums = [jnp.sum(part, axis=1, keepdims=True) for part in weights]
+        for (i, lo, hi, _), part, top, total in zip(near, weights, tops, sums):
+            rows = slice(i * BLK, (i + 1) * BLK)
+            mix_v[h, rows, :] = mix(part, kv_v[h, 1, lo:hi, :])
+            top_v[h, rows, :] = jnp.broadcast_to(top, (BLK, HEAD))
+            sum_v[h, rows, :] = jnp.broadcast_to(total, (BLK, HEAD))
+
+    for h in range(4):
+        run(has_last1 & low, lambda h=h: recv(kv_v.at[h, 0, pl.ds(BLK, 2 * BLK), :], halo_slots[h][0]))
+        send(kv_v.at[h, 0, pl.ds(2 * BLK, BLK), :], kv_v.at[h, 0, pl.ds(0, BLK), :], halo_slots[h][1], next1,
+             low & has_last1 & has_next1)
+    for h in range(4):
+        run(has_last1 & high, lambda h=h: recv(kv_v.at[h, 0, pl.ds(BLK, 2 * BLK), :], halo_slots[h][0]))
+        run(has_last1, lambda h=h: recv(kv_v.at[h, 1, pl.ds(BLK, 2 * BLK), :], halo_slots[h][2]))
         for kind in range(2):
-            run(has_last1, lambda h=h, kind=kind: recv(kv_v.at[h, kind, pl.ds(BLK, 2 * BLK), :], halo_slots[h][2 * kind]))
             run(has_last2, lambda h=h, kind=kind: recv(kv_v.at[h, kind, pl.ds(0, BLK), :], halo_slots[h][2 * kind + 1]))
+        scores = [scored(h, i, kv_v[h, 0, lo:hi, :], first) for i, lo, hi, first in far]
+        before = [top_v[h, i * BLK:(i + 1) * BLK, :] for i in range(2)]
+        tops = [jnp.maximum(jnp.max(part, axis=1, keepdims=True), old) for part, old in zip(scores, before)]
+        weights = [
+            jnp.exp2(part - jnp.concatenate([top] * (part.shape[1] // HEAD), axis=1)) for part, top in zip(scores, tops)
+        ]
+        sums = [jnp.sum(part, axis=1, keepdims=True) for part in weights]
+        mixed = [mix(part, kv_v[h, 1, lo:hi, :]) for part, (_, lo, hi, _) in zip(weights, far)]
         for i in range(2):
-            keys = kv_v[h, 0, i * BLK:(i + 4) * BLK, :]
-            values = kv_v[h, 1, i * BLK:(i + 4) * BLK, :]
-            scores = lax.dot_general(
-                q_v[h, i * BLK:(i + 1) * BLK, :], keys, (((1,), (1,)), ((), ())),
-                preferred_element_type=jnp.float32,
-            )
-            scores = scores * (1.0 / math.sqrt(HEAD)) + bias_v[i]
-            top = jnp.max(scores, axis=1, keepdims=True)
-            weights = jnp.exp(scores - top)
-            total = jnp.sum(weights, axis=1, keepdims=True)
-            mixed = jnp.dot(weights.astype(jnp.bfloat16), values, preferred_element_type=jnp.float32)
-            blo_v[h, i * BLK:(i + 1) * BLK, :] = (mixed / total).astype(jnp.bfloat16)
+            rows = slice(i * BLK, (i + 1) * BLK)
+            shrink = jnp.exp2(before[i] - tops[i])
+            total = sum_v[h, rows, :] * shrink + sums[i]
+            blo_v[h, rows, :] = ((mix_v[h, rows, :] * shrink + mixed[i]) / total).astype(jnp.bfloat16)
         send(blo_v.at[h], bl_v.at[4 * j + h], bl_slots[h], ph_next, ph + 1 < phases)
         send(blo_v.at[h, theirs, :], bls_v.at[h], bls_slots[h], sibling)
 
@@ -453,8 +496,8 @@
         out_ref[:, n:n + step] = (x_v[mine, n:n + step].astype(jnp.float32) + update).astype(jnp.bfloat16)
 
     pl.when(late_help)(help_halo)
-    pl.when(late_pass)(pass_residual)
-    for made, when in pending + rel_copies + [(made, has_pass if k > 1 else pass_all) for k, made in enumerate(res_copies)]:
+    pl.when(turn_pass)(pass_residual)
+    for made, when in pending + rel_copies + far_copies + [(made, turn_pass) for made in res_copies]:
         if when is None:
             made.wait_send()
         else:
@@ -496,8 +539,12 @@
                 pltpu.VMEM((5, 8, BLK), jnp.float32),
                 pltpu.VMEM((2, BLK, 4 * BLK), jnp.float32),
                 pltpu.VMEM((4, 2 * BLK, HEAD), jnp.bfloat16),
+                pltpu.VMEM((4, BLK, HEAD), jnp.bfloat16),
                 pltpu.VMEM((4, BLK // 4, width), jnp.bfloat16),
                 pltpu.VMEM((2 * BLK, HEAD), jnp.float32),
+                pltpu.VMEM((4, 2 * BLK, HEAD), jnp.float32),
+                pltpu.VMEM((4, 2 * BLK, HEAD), jnp.float32),
+                pltpu.VMEM((4, 2 * BLK, HEAD), jnp.float32),
                 pltpu.SemaphoreType.DMA((n_slots,)),
                 pltpu.SemaphoreType.DMA((n_slots,)),
                 pltpu.SemaphoreType.DMA((16,)),

time: 246 us -> 223 us (0.907); the launches traced: 243 us -> 223 us
  Pallas kernels: 240 us -> 220 us
    pallas_call x1, Pallas kernels: 240 us -> 220 us  [local(): pl.pallas_call(functools.partial(kernel, phases, chips), out_shape=jax.Sh...]
where the time goes in v4:
time: 223 us
  Pallas kernels  220 us (99%)
  local copies, waits for them, and re-layouts  2.48 us (1%)
    pallas_call x1, Pallas kernels, local(): pl.pallas_call(functools.partial(kernel, phases, chips), out_shape=jax.Sh...  220 us

profile of v4, /device:TPU:63, one launch (start us, length us, event | category | flops | bytes accessed | tf_op | source)
XLA Modules:
  0.0 223.3 jit_solution(6282243981288459536)
XLA Ops:
  0.0 0.7 convert_bitcast_fusion
  0.7 0.6 broadcast_in_dim.8.seg_in
  1.3 220.2 %shard_map.55 = bf16[128,2048]{1,0:T(8,128)(2,1)} custom-call(bf16[128,2048]{1,0:T(8,128)(2,1)} %bitcast.10, f32[8,128]{1,0:T(8,128)} %broadcast_in_dim.8.seg_in, bf16[2048,1024]{1,0:T(8,128)(2,1)} %bitcast.7, bf16[64,2048]{1,0:T(8,128)(2,1)} %bitcast.11, bf16[8,128,2048]{2,1,0:T(8,128)(2,1)} %bitcast.8), custom_call_target="tpu_custom_call" | custom-call | tf_op jit(solution)/shard_map/pallas_call | solution.py:522
  221.5 1.9 copy.7

commit v5 on v4

--- a/solution.py
+++ b/solution.py
@@ -16,7 +16,7 @@
 
 def kernel(
     phases, chips, x_in, seg_in, wq_in, wkv_in, wo_in, out_ref,
-    x_v, acc, wq_v, wkv_v, wo_v, wop_v, q_v, kv_v, bl_v, blo_v, bls_v, seg_v, bias_v, rel_v, far_v, res_v, sq_v, mix_v, top_v, sum_v,
+    x_v, acc, wq_v, wkv_v, wo_v, wop_v, q_v, kv_v, bl_v, blo_v, bls_v, seg_v, bias_v, rel_v, far_v, sq_v, mix_v, top_v, sum_v,
     ssem, rsem, lsem, go_sem,
 ):
     width = x_v.shape[1]
@@ -53,15 +53,32 @@
     has_helper, has_helped = ph > 0, ph != RING - 1
     helper = jnp.where(ph == RING, 2 * RING - 1, jnp.maximum(ph - 1, 0))
     helped = jnp.where(early_help, RING, jnp.minimum(ph + 1, phases - 1))
-    res_out, res_in = (ph >= 1) & (ph + 1 < phases), ph >= 2
-    turn_pass = ph == 0
+    row_end = z == RING - 1
+    helper_chip = jnp.where(row_end, jnp.minimum(p + RING, chips - 1), p)
+    helped_chip = jnp.where(row_end, jnp.maximum(p - RING, 0), p)
+    helped_to1, helped_to2 = jnp.minimum(helped_chip + 1, chips - 1), jnp.minimum(helped_chip + 2, chips - 1)
+    has_helped = has_helped & (jnp.logical_not(row_end) | (p >= RING))
+    helped1, helped2 = has_helped & (helped_chip + 1 < chips), has_helped & (helped_chip + 2 < chips)
+
+    def helper_of(chip):
+        chip = jnp.maximum(chip, 0)
+        return at(helper, jnp.where(chip % RING == RING - 1, jnp.minimum(chip + RING, chips - 1), chip))
+
+    res_out, res_in = ph + 2 < phases, ph >= 2
+    ph_next2, ph_prev2 = at(jnp.minimum(ph + 2, phases - 1), p), at(jnp.maximum(ph - 2, 0), p)
     low, high = ph < RING, ph >= RING
-    far_chip = at(jnp.minimum(ph + RING, phases - 1), chip_at(0, -1))
-    far_from, far_phase = chip_at(0, 1), jnp.maximum(ph - RING, 0)
+    def far_of(chip):
+        chip = jnp.clip(chip, 0, chips - 1)
+        crossing = chip % RING >= 2
+        row = jnp.minimum(chip // RING + jnp.where(crossing, 1, 0), RING - 1)
+        return at(jnp.minimum(ph + RING, phases - 1), row * RING + (chip % RING + RING - 1) % RING)
+
+    far_chip, far_back = far_of(p), far_of(p - 2)
+    far_z = (z + 1) % RING
+    far_row = y - jnp.where(far_z >= 2, 1, 0)
+    far_from, far_phase = jnp.maximum(far_row, 0) * RING + far_z, jnp.maximum(ph - RING, 0)
     far_to = jnp.minimum(far_from + 2, chips - 1)
-    does_far = high & (far_from + 2 < chips)
-    two_back = jnp.maximum(p - 2, 0)
-    far_back = at(jnp.minimum(ph + RING, phases - 1), (two_back // RING) * RING + (two_back + RING - 1) % RING)
+    does_far = high & (far_row >= 0) & (far_from + 2 < chips)
     turn_out, turn_in = ph == RING - 1, ph == RING
 
     barrier = pltpu.get_barrier_semaphore()
@@ -73,12 +90,10 @@
         (ph_next, ph + 1 < phases), (ph_prev, ph > 0), (at(goer, p), has_under), (at(ph + RING - 1, p), goes_late), (at(jnp.minimum(ph + RING, phases - 1), p), goes_early),
         (far_chip, low & has_next2), (far_back, low & has_last2),
         (at(far_phase, far_from), does_far), (at(far_phase, far_to), does_far),
-        (at(helper, p), has_helper), (at(helped, p), has_helped),
-        (at(helped, jnp.minimum(p + 1, chips - 1)), has_helped & has_next1),
-        (at(helped, jnp.minimum(p + 2, chips - 1)), has_helped & has_next2),
-        (at(helper, jnp.maximum(p - 1, 0)), has_helper & has_last1),
-        (at(helper, jnp.maximum(p - 2, 0)), has_helper & has_last2),
-        (at(0, p), turn_out | turn_in), (at(RING - 1, p), turn_pass), (at(RING, p), turn_pass),
+        (helper_of(p), has_helper & has_next1), (at(helped, helped_chip), helped1),
+        (at(helped, helped_to1), helped1), (at(helped, helped_to2), helped2),
+        (helper_of(p - 1), has_helper & has_last1), (helper_of(p - 2), has_helper & has_last2),
+        (ph_next2, res_out), (ph_prev2, res_in),
         (at(jnp.minimum(ph + 1, phases - 1), chip_at(0, -1)), turn_out),
         (at(jnp.maximum(ph - 1, 0), chip_at(0, 1)), turn_in),
     ):
@@ -137,17 +152,19 @@
     wo_load = load(wo_in, wo_v)
 
     halo_slots = [[next(slots) for _ in range(4)] for _ in range(4)]
-    rel_slots = [next(slots) for _ in range(4)]
+    rel_slots = [[next(slots), next(slots)] for _ in range(4)]
+    late_slots = [next(slots) for _ in range(4)]
     far_slots = [next(slots) for _ in range(4)]
     helped_high = helped >= RING
     rel_copies = []
     for h in range(4):
-        rel_copies.append((copy(rel_v.at[h], kv_v.at[h, 1, pl.ds(BLK, 2 * BLK), :], halo_slots[h][2],
-                                at(helped, jnp.minimum(p + 1, chips - 1))),
-                           has_helped & has_next1 & (True if h > 0 else jnp.logical_not(helped_high))))
+        needed = helped1 & (True if h > 0 else jnp.logical_not(helped_high))
+        for b, slot in enumerate((halo_slots[h][2], late_slots[h])):
+            rel_copies.append((copy(rel_v.at[h, pl.ds(b * BLK, BLK), :], kv_v.at[h, 1, pl.ds((b + 1) * BLK, BLK), :],
+                                    slot, at(helped, helped_to1)), needed))
     for h in range(1, 4):
         rel_copies.append((copy(rel_v.at[h, pl.ds(BLK, BLK), :], kv_v.at[h, 1, pl.ds(0, BLK), :], halo_slots[h][3],
-                                at(helped, jnp.minimum(p + 2, chips - 1))), has_helped & has_next2 & helped_high))
+                                at(helped, helped_to2)), helped2 & helped_high))
     far_copies = [
         (copy(far_v.at[h], kv_v.at[h, 1, pl.ds(0, BLK), :], halo_slots[h][3], at(far_phase, far_to)), does_far)
         for h in range(4)
@@ -155,13 +172,14 @@
 
     def help_halo():
         for h in range(4):
-            @pl.when(rel_copies[h][1])
+            @pl.when(rel_copies[2 * h][1])
             def _(h=h):
-                recv(rel_v.at[h], rel_slots[h])
-                rel_copies[h][0].start()
+                for b in range(2):
+                    recv(rel_v.at[h, pl.ds(b * BLK, BLK), :], rel_slots[h][b])
+                    rel_copies[2 * h + b][0].start()
 
             if h > 0:
-                pl.when(rel_copies[h + 3][1])(rel_copies[h + 3][0].start)
+                pl.when(rel_copies[h + 7][1])(rel_copies[h + 7][0].start)
 
     def help_far():
         for h in range(4):
@@ -186,7 +204,6 @@
     x_slot = next(slots)
     x_prev_slots = [next(slots) for _ in range(4)]
     x_relay_slots = [next(slots) for _ in range(4)]
-    res_slots = [next(slots) for _ in range(4)]
     x_load = pltpu.make_async_copy(x_in, x_v.at[mine], lsem.at[len(local)])
     x_direct = copy(x_in, x_v.at[mine], x_slot, sibling)
 
@@ -291,20 +308,13 @@
     def go(phase):
         pl.semaphore_signal(go_sem, inc=1, device_id=at(jnp.minimum(phase, phases - 1), p), device_id_type=MESH)
 
-    piece = BLK // 4
+    piece = width // 4
 
     def mine_at(k):
-        return x_v.at[pl.ds(pl.multiple_of(j * BLK + k * piece, piece), piece), :]
+        return x_v.at[mine, pl.ds(k * piece, piece)]
 
     def theirs_at(k):
-        return x_v.at[pl.ds(pl.multiple_of((1 - j) * BLK + k * piece, piece), piece), :]
-
-    res_copies = [copy(res_v.at[k], mine_at(k), x_prev_slots[k], at(RING, p)) for k in range(1, 4)]
-
-    def pass_residual():
-        for k in range(1, 4):
-            recv(res_v.at[k], res_slots[k])
-            res_copies[k - 1].start()
+        return x_v.at[theirs, pl.ds(k * piece, piece)]
 
     pl.when(goes_early)(lambda: go(ph + RING))
     pl.when(does_far & (ph >= RING + 2))(help_far)
@@ -317,11 +327,19 @@
         relays.append(copy(wop_v.at[4 * j + k], wop_v.at[4 * j + k], wop_relay[k], sibling))
     x_relays = [copy(mine_at(k), mine_at(k), x_relay_slots[k], sibling) for k in range(4)]
 
-    @pl.when(ph > 0)
-    def _():
-        for k in range(4):
+    def take_wop(first):
+        for k in (first, first + 1):
             recv(wop_v.at[4 * j + k], wop_slots[k])
             relays[k].start()
+
+    def get_wop(first):
+        for k in (first, first + 1):
+            recv(wop_v.at[4 * (1 - j) + k], wop_relay[k])
+
+    pl.when(ph > 0)(lambda: take_wop(0))
+    pl.when(ph > 1)(lambda: take_wop(2))
+    pl.when(ph > 0)(lambda: get_wop(0))
+    pl.when(ph > 1)(lambda: get_wop(2))
 
     @pl.when(ph < 2)
     def _():
@@ -345,8 +363,6 @@
 
     @pl.when(ph > 0)
     def _():
-        for k in range(4):
-            recv(wop_v.at[4 * (1 - j) + k], wop_relay[k])
         mine_head, their_head = 4 * j, 4 * (1 - j)
         def take(h):
             recv(bl_v.at[mine_head + h], bl_slots[h])
@@ -375,11 +391,14 @@
                 recv(mine_at(k), x_prev_slots[k])
                 x_relays[k].start()
 
+        pl.when(ph == 1)(lambda: take_wop(2))
         recv(bl_v.at[their_head], bl_relay_slots[0])
         recv(bl_v.at[their_head + 1], bl_relay_slots[1])
         take(2)
         project_heads(0)
         take(3)
+        pl.when(ph == 1)(lambda: get_wop(2))
+
         recv(bl_v.at[their_head + 2], bl_relay_slots[2])
         recv(bl_v.at[their_head + 3], bl_relay_slots[3])
 
@@ -400,38 +419,61 @@
     square = jnp.sum(sq_v[...], axis=1, keepdims=True)
     scale_rows = lax.rsqrt(square * (1.0 / width) + 1e-05)
 
-    for k in range(4):
-        send(mine_at(k), mine_at(k), x_prev_slots[k], ph_next, res_out if k == 0 else res_out & jnp.logical_not(turn_out))
-        if k > 0:
-            send(mine_at(k), res_v.at[k], res_slots[k], at(0, p), turn_out)
     stream = x_v[...]
 
     def project(weights):
         return (jnp.dot(stream, weights, preferred_element_type=jnp.float32) * scale_rows).astype(jnp.bfloat16)
 
-    for kind in (1, 0):
-        for t in range(2):
-            made = project(wkv_v[2 * t + kind])
-            kv_v[2 * t, kind, 3 * BLK:5 * BLK, :] = made[:, :HEAD]
-            kv_v[2 * t + 1, kind, 3 * BLK:5 * BLK, :] = made[:, HEAD:]
-            for h in (2 * t, 2 * t + 1):
-                both = kv_v.at[h, kind, pl.ds(3 * BLK, 2 * BLK), :]
-                odd = kv_v.at[h, kind, pl.ds(4 * BLK, BLK), :]
-                to_next1, to_next2 = kv_v.at[h, kind, pl.ds(BLK, 2 * BLK), :], kv_v.at[h, kind, pl.ds(0, BLK), :]
-                if kind == 0:
-                    send(both, to_next1, halo_slots[h][0], next1, has_next1)
-                    send(odd, to_next2, halo_slots[h][1], next2, has_next2 & high)
-                    continue
-                straight = is_first | high if h < 1 else is_first
-                send(both, rel_v.at[h], rel_slots[h], at(helper, p), has_next1 & jnp.logical_not(straight))
-                send(both, to_next1, halo_slots[h][2], next1, straight & has_next1)
-                if h < 1:
-                    send(odd, to_next2, halo_slots[h][3], next2, has_next2 & high)
-                send(odd, far_v.at[h], far_slots[h], far_chip, has_next2 & low)
-    for t in range(2):
-        made = project(wq_v[t])
-        q_v[2 * t] = made[:, :HEAD]
-        q_v[2 * t + 1] = made[:, HEAD:]
+    def own_blocks(kind, h, first, count):
+        return kv_v.at[h, kind, pl.ds((3 + first) * BLK, count * BLK), :]
+
+    def begin(when, chosen):
+        @pl.when(when)
+        def _():
+            for made in chosen:
+                made.start()
+
+        pending.extend((made, when) for made in chosen)
+
+    def ahead(kind, heads):
+        return [
+            copy(own_blocks(kind, h, 1, 1), kv_v.at[h, kind, pl.ds(0, BLK), :], halo_slots[h][2 * kind + 1], next2)
+            for h in heads
+        ]
+
+    def start_keys(heads):
+        begin(has_next1, [
+            copy(own_blocks(0, h, 0, 2), kv_v.at[h, 0, pl.ds(BLK, 2 * BLK), :], halo_slots[h][0], next1) for h in heads
+        ])
+        begin(has_next2 & high, ahead(0, heads))
+
+    def start_values():
+        direct, around = [], []
+        for h in range(4):
+            for b, slot in enumerate((halo_slots[h][2], late_slots[h])):
+                direct.append(copy(own_blocks(1, h, b, 1), kv_v.at[h, 1, pl.ds((b + 1) * BLK, BLK), :], slot, next1))
+                around.append(
+                    copy(own_blocks(1, h, b, 1), rel_v.at[h, pl.ds(b * BLK, BLK), :], rel_slots[h][b], helper_of(p))
+                )
+        begin(has_next1 & high, around[2:] + direct[:2])
+        begin(has_next1 & low & jnp.logical_not(is_first), around)
+        begin(has_next1 & is_first, direct)
+        begin(has_next2 & low, [
+            copy(own_blocks(1, h, 1, 1), far_v.at[h], far_slots[h], far_chip) for h in range(4)
+        ])
+        begin(has_next2 & high, ahead(1, (0,)))
+
+    for kind in (0, 1):
+        made = project(jnp.concatenate([wkv_v[kind], wkv_v[2 + kind]], axis=1))
+        for h in range(4):
+            kv_v[h, kind, 3 * BLK:5 * BLK, :] = made[:, h * HEAD:(h + 1) * HEAD]
+        if kind == 0:
+            start_keys((0,))
+    start_values()
+    start_keys((1, 2, 3))
+    made = project(jnp.concatenate([wq_v[0], wq_v[1]], axis=1))
+    for h in range(4):
+        q_v[h] = made[:, h * HEAD:(h + 1) * HEAD]
 
     bls_slots = [next(slots) for _ in range(4)]
     factor = math.log2(math.e) / math.sqrt(HEAD)
@@ -463,7 +505,8 @@
              low & has_last1 & has_next1)
     for h in range(4):
         run(has_last1 & high, lambda h=h: recv(kv_v.at[h, 0, pl.ds(BLK, 2 * BLK), :], halo_slots[h][0]))
-        run(has_last1, lambda h=h: recv(kv_v.at[h, 1, pl.ds(BLK, 2 * BLK), :], halo_slots[h][2]))
+        run(has_last1, lambda h=h: recv(kv_v.at[h, 1, pl.ds(BLK, BLK), :], halo_slots[h][2]))
+        run(has_last1, lambda h=h: recv(kv_v.at[h, 1, pl.ds(2 * BLK, BLK), :], late_slots[h]))
         for kind in range(2):
             run(has_last2, lambda h=h, kind=kind: recv(kv_v.at[h, kind, pl.ds(0, BLK), :], halo_slots[h][2 * kind + 1]))
         scores = [scored(h, i, kv_v[h, 0, lo:hi, :], first) for i, lo, hi, first in far]
@@ -479,7 +522,10 @@
             shrink = jnp.exp2(before[i] - tops[i])
             total = sum_v[h, rows, :] * shrink + sums[i]
             blo_v[h, rows, :] = ((mix_v[h, rows, :] * shrink + mixed[i]) / total).astype(jnp.bfloat16)
-        send(blo_v.at[h], bl_v.at[4 * j + h], bl_slots[h], ph_next, ph + 1 < phases)
+        blended_last = copy(blo_v.at[h], bl_v.at[4 * j + h], bl_slots[h], ph_next)
+        pl.when(ph + 1 < phases)(blended_last.start)
+        if h < 3:
+            pending.append((blended_last, ph + 1 < phases))
         send(blo_v.at[h, theirs, :], bls_v.at[h], bls_slots[h], sibling)
 
     pl.when(goes_late)(lambda: go(ph + RING - 1))
@@ -494,10 +540,12 @@
         update = jnp.dot(own, first, preferred_element_type=jnp.float32)
         update = update + jnp.dot(other, second, preferred_element_type=jnp.float32)
         out_ref[:, n:n + step] = (x_v[mine, n:n + step].astype(jnp.float32) + update).astype(jnp.bfloat16)
+    pl.when(ph + 1 < phases)(blended_last.wait_send)
+    for k in range(4):
+        send(out_ref.at[:, pl.ds(k * piece, piece)], mine_at(k), x_prev_slots[k], ph_next2, res_out)
 
     pl.when(late_help)(help_halo)
-    pl.when(turn_pass)(pass_residual)
-    for made, when in pending + rel_copies + far_copies + [(made, turn_pass) for made in res_copies]:
+    for made, when in pending + rel_copies + far_copies:
         if when is None:
             made.wait_send()
         else:
@@ -518,7 +566,7 @@
         rows_dev = w_keyval.shape[1]
         seg = jnp.broadcast_to(segment_ids.astype(jnp.float32), (8, BLK))
         any_space = pl.BlockSpec(memory_space=pl.ANY)
-        n_slots = 128
+        n_slots = 144
         made = pl.pallas_call(
             functools.partial(kernel, phases, chips),
             out_shape=jax.ShapeDtypeStruct((BLK, width), jnp.bfloat16),
@@ -540,7 +588,6 @@
                 pltpu.VMEM((2, BLK, 4 * BLK), jnp.float32),
                 pltpu.VMEM((4, 2 * BLK, HEAD), jnp.bfloat16),
                 pltpu.VMEM((4, BLK, HEAD), jnp.bfloat16),
-                pltpu.VMEM((4, BLK // 4, width), jnp.bfloat16),
                 pltpu.VMEM((2 * BLK, HEAD), jnp.float32),
                 pltpu.VMEM((4, 2 * BLK, HEAD), jnp.float32),
                 pltpu.VMEM((4, 2 * BLK, HEAD), jnp.float32),

time: 223 us -> 215 us (0.964); the launches traced: 223 us -> 213 us
  Pallas kernels: 220 us -> 210 us
    pallas_call x1, Pallas kernels: 220 us -> 210 us  [local(): pl.pallas_call(functools.partial(kernel, phases, chips), out_shape=jax.Sh...]
where the time goes in v5:
time: 215 us; the launch traced here: 213 us
  Pallas kernels  210 us (98%)
  local copies, waits for them, and re-layouts  2.48 us (1%)
    pallas_call x1, Pallas kernels, local(): pl.pallas_call(functools.partial(kernel, phases, chips), out_shape=jax.Sh...  210 us

profile of v5, /device:TPU:63, one launch (start us, length us, event | category | flops | bytes accessed | tf_op | source)
XLA Modules:
  0.0 212.9 jit_solution(14561895856355987841)
XLA Ops:
  0.0 0.7 convert_bitcast_fusion
  0.7 0.6 broadcast_in_dim.8.seg_in
  1.3 209.8 %shard_map.55 = bf16[128,2048]{1,0:T(8,128)(2,1)} custom-call(bf16[128,2048]{1,0:T(8,128)(2,1)} %bitcast.10, f32[8,128]{1,0:T(8,128)} %broadcast_in_dim.8.seg_in, bf16[2048,1024]{1,0:T(8,128)(2,1)} %bitcast.7, bf16[64,2048]{1,0:T(8,128)(2,1)} %bitcast.11, bf16[8,128,2048]{2,1,0:T(8,128)(2,1)} %bitcast.8), custom_call_target="tpu_custom_call" | custom-call | tf_op jit(solution)/shard_map/pallas_call | solution.py:570
  211.0 1.9 copy.7

commit v6 on v5

--- a/solution.py
+++ b/solution.py
@@ -16,7 +16,7 @@
 
 def kernel(
     phases, chips, x_in, seg_in, wq_in, wkv_in, wo_in, out_ref,
-    x_v, acc, wq_v, wkv_v, wo_v, wop_v, q_v, kv_v, bl_v, blo_v, bls_v, seg_v, bias_v, rel_v, far_v, sq_v, mix_v, top_v, sum_v,
+    x_v, acc, wq_v, wkv_v, wo_v, wop_v, q_v, kv_v, bl_v, blo_v, bls_v, seg_v, bias_v, rel_v, far_v, via_v, sq_v, mix_v, top_v, sum_v,
     ssem, rsem, lsem, go_sem,
 ):
     width = x_v.shape[1]
@@ -93,7 +93,7 @@
         (helper_of(p), has_helper & has_next1), (at(helped, helped_chip), helped1),
         (at(helped, helped_to1), helped1), (at(helped, helped_to2), helped2),
         (helper_of(p - 1), has_helper & has_last1), (helper_of(p - 2), has_helper & has_last2),
-        (ph_next2, res_out), (ph_prev2, res_in),
+        (ph_next2, res_out), (ph_prev2, res_in), (at(RING - 1, p), is_first), (at(0, p), turn_out),
         (at(jnp.minimum(ph + 1, phases - 1), chip_at(0, -1)), turn_out),
         (at(jnp.maximum(ph - 1, 0), chip_at(0, 1)), turn_in),
     ):
@@ -142,7 +142,7 @@
 
     own_rows = pl.ds(pl.multiple_of(c * rows_dev, rows_dev), rows_dev)
     shard_loads = [load(wkv_in.at[:, columns(j, t)], wkv_v.at[t, own_rows, :]) for t in range(4)]
-    seg_load = load(seg_in, seg_v.at[3 + j])
+    seg_v[3 + j] = jnp.broadcast_to(seg_in[...].astype(jnp.float32), seg_v.shape[1:])
     mine = pl.ds(pl.multiple_of(j * BLK, BLK), BLK)
     theirs = pl.ds(pl.multiple_of((1 - j) * BLK, BLK), BLK)
     wq_loads = [
@@ -192,14 +192,24 @@
 
     for t in range(4):
         send(wkv_in.at[:, columns(1 - j, t)], wkv_v.at[t, own_rows, :], shard_slots[t], sibling)
-    send(seg_in, seg_v.at[3 + j], seg_slots[0], sibling)
+    send(seg_v.at[3 + j], seg_v.at[3 + j], seg_slots[0], sibling)
 
     wop_slots = [next(slots) for _ in range(4)]
 
     def send_wop(when, devices):
         for k in range(4):
-            send(wo_in.at[4 * j + k], wop_v.at[4 * j + k], wop_slots[k], devices[k // 2], when)
-
+            send(wo_in.at[4 * j + k], wop_v.at[4 * j + k], wop_slots[k], devices[k // 2],
+                 when & jnp.logical_not(is_first) if k == 3 else when)
+
+    via_slots = [next(slots), next(slots)]
+    via_mid = copy(via_v, via_v, via_slots[1], at(2, p))
+    via_end = copy(via_v, wop_v.at[4 * j + 3], wop_slots[3], at(1, p))
+
+    def pass_via(slot, made):
+        recv(via_v, slot)
+        made.start()
+
+    send(wo_in.at[4 * j + 3], via_v, via_slots[0], at(RING - 1, p), is_first)
     send_wop((ph + 1 < phases) & jnp.logical_not(turn_out), (ph_next, ph_next))
     x_slot = next(slots)
     x_prev_slots = [next(slots) for _ in range(4)]
@@ -250,7 +260,6 @@
         recv(slab(far, g["tile"], 1), slot[2])
         recv(slab(far, g["tile"] + 1, 1), slot[3])
 
-    seg_load.wait()
     recv(seg_v.at[4 - j], seg_slots[0])
     send(seg_v.at[pl.ds(3, 2)], seg_v.at[pl.ds(1, 2)], seg_slots[1], next1, has_next1)
     send(seg_v.at[4], seg_v.at[0], seg_slots[2], next2, has_next2)
@@ -291,6 +300,7 @@
         ring_send(g, g["sec"], g["sslot"][1], 1)
     for g in sets:
         ring_forward(g, g["sec"], g["sslot"][0], g["chip"](0, -1), g["chip"](0, 1))
+    pl.when(turn_out)(lambda: pass_via(via_slots[0], via_mid))
     for g in sets:
         ring_end(g, g["pslot"], g["chip"](2, 0))
         ring_send(g, g["sec"], g["sslot"][2], 2)
@@ -298,6 +308,7 @@
         for g in sets:
             ring_forward(g, g["sec"], g["sslot"][dp], g["chip"](dp, -1), g["chip"](dp, 1))
 
+    pl.when(ph == 2)(lambda: pass_via(via_slots[1], via_end))
     for dp in (0, -1, 1, 2):
         for g in sets:
             ring_end(g, g["sslot"][dp], g["chip"](dp, 2))
@@ -545,7 +556,7 @@
         send(out_ref.at[:, pl.ds(k * piece, piece)], mine_at(k), x_prev_slots[k], ph_next2, res_out)
 
     pl.when(late_help)(help_halo)
-    for made, when in pending + rel_copies + far_copies:
+    for made, when in pending + rel_copies + far_copies + [(via_mid, turn_out), (via_end, ph == 2)]:
         if when is None:
             made.wait_send()
         else:
@@ -564,13 +575,12 @@
     def local(inputs, segment_ids, w_query, w_keyval, w_out):
         width = inputs.shape[2]
         rows_dev = w_keyval.shape[1]
-        seg = jnp.broadcast_to(segment_ids.astype(jnp.float32), (8, BLK))
         any_space = pl.BlockSpec(memory_space=pl.ANY)
         n_slots = 144
         made = pl.pallas_call(
             functools.partial(kernel, phases, chips),
             out_shape=jax.ShapeDtypeStruct((BLK, width), jnp.bfloat16),
-            in_specs=[any_space] * 5,
+            in_specs=[any_space, pl.BlockSpec(memory_space=pltpu.VMEM)] + [any_space] * 3,
             out_specs=pl.BlockSpec(memory_space=pltpu.VMEM),
             scratch_shapes=[
                 pltpu.VMEM((2 * BLK, width), jnp.bfloat16),
@@ -588,6 +598,7 @@
                 pltpu.VMEM((2, BLK, 4 * BLK), jnp.float32),
                 pltpu.VMEM((4, 2 * BLK, HEAD), jnp.bfloat16),
                 pltpu.VMEM((4, BLK, HEAD), jnp.bfloat16),
+                pltpu.VMEM((HEAD, width), jnp.bfloat16),
                 pltpu.VMEM((2 * BLK, HEAD), jnp.float32),
                 pltpu.VMEM((4, 2 * BLK, HEAD), jnp.float32),
                 pltpu.VMEM((4, 2 * BLK, HEAD), jnp.float32),
@@ -601,7 +612,7 @@
                 collective_id=0, has_side_effects=True, vmem_limit_bytes=56 * 1024 * 1024
             ),
         )(
-            inputs.reshape(BLK, width), seg, w_query.reshape(width, -1),
+            inputs.reshape(BLK, width), segment_ids, w_query.reshape(width, -1),
             w_keyval.reshape(rows_dev, -1), w_out.reshape(8, HEAD, width),
         )
         return made.reshape(1, 1, BLK, width)

time: 215 us -> 213 us (level)
  no operation moved by 1% of the time
where the time goes in v6:
time: 213 us; the launch traced here: 211 us
  Pallas kernels  209 us (98%)
    pallas_call x1, Pallas kernels, local(): pl.pallas_call(functools.partial(kernel, phases, chips), out_shape=jax.Sh...  209 us

profile of v6, /device:TPU:63, one launch (start us, length us, event | category | flops | bytes accessed | tf_op | source)
XLA Modules:
  0.0 211.0 jit_solution(15298492954849482215)
XLA Ops:
  0.0 209.1 %shard_map.55 = bf16[128,2048]{1,0:T(8,128)(2,1)} custom-call(bf16[128,2048]{1,0:T(8,128)(2,1)} %bitcast.8, s32[1,128]{1,0:T(1,128)} %seg_in.1, bf16[2048,1024]{1,0:T(8,128)(2,1)} %bitcast.5, bf16[64,2048]{1,0:T(8,128)(2,1)} %bitcast.9, bf16[8,128,2048]{2,1,0:T(8,128)(2,1)} %bitcast.6), custom_call_target="tpu_custom_call" | custom-call | tf_op jit(solution)/shard_map/pallas_call | solution.py:580
  209.1 1.9 copy.7

commit v7 on v6

--- a/solution.py
+++ b/solution.py
@@ -16,7 +16,7 @@
 
 def kernel(
     phases, chips, x_in, seg_in, wq_in, wkv_in, wo_in, out_ref,
-    x_v, acc, wq_v, wkv_v, wo_v, wop_v, q_v, kv_v, bl_v, blo_v, bls_v, seg_v, bias_v, rel_v, far_v, via_v, sq_v, mix_v, top_v, sum_v,
+    x_v, acc, wq_v, wkv_v, wo_v, wop_v, q_v, kv_v, bl_v, blo_v, bls_v, seg_v, bias_v, rel_v, far_v, via_v, res_v, sq_v, mix_v, top_v, sum_v,
     ssem, rsem, lsem, go_sem,
 ):
     width = x_v.shape[1]
@@ -65,6 +65,14 @@
         return at(helper, jnp.where(chip % RING == RING - 1, jnp.minimum(chip + RING, chips - 1), chip))
 
     res_out, res_in = ph + 2 < phases, ph >= 2
+    res_even = res_out & (ph % RING == 0)
+    res_direct = res_out & (ph % RING != 0)
+    res_via = jnp.minimum(ph + RING - 1, phases - 1)
+    passes = ph % RING == RING - 1
+    pass_from = jnp.maximum(ph - RING + 1, 0)
+    pass_to = jnp.minimum(pass_from + 2, phases - 1)
+    res_back = jnp.minimum(ph + 1, phases - 1)
+    res_around = ph % RING == 2
     ph_next2, ph_prev2 = at(jnp.minimum(ph + 2, phases - 1), p), at(jnp.maximum(ph - 2, 0), p)
     low, high = ph < RING, ph >= RING
     def far_of(chip):
@@ -93,7 +101,9 @@
         (helper_of(p), has_helper & has_next1), (at(helped, helped_chip), helped1),
         (at(helped, helped_to1), helped1), (at(helped, helped_to2), helped2),
         (helper_of(p - 1), has_helper & has_last1), (helper_of(p - 2), has_helper & has_last2),
-        (ph_next2, res_out), (ph_prev2, res_in), (at(RING - 1, p), is_first), (at(0, p), turn_out),
+        (ph_next2, res_direct), (ph_prev2, res_in & jnp.logical_not(res_around)),
+        (at(res_via, p), res_even), (at(pass_from, p), passes), (at(pass_to, p), passes),
+        (at(res_back, p), res_around), (at(RING - 1, p), is_first), (at(0, p), turn_out),
         (at(jnp.minimum(ph + 1, phases - 1), chip_at(0, -1)), turn_out),
         (at(jnp.maximum(ph - 1, 0), chip_at(0, 1)), turn_in),
     ):
@@ -214,6 +224,7 @@
     x_slot = next(slots)
     x_prev_slots = [next(slots) for _ in range(4)]
     x_relay_slots = [next(slots) for _ in range(4)]
+    res_slots = [next(slots) for _ in range(4)]
     x_load = pltpu.make_async_copy(x_in, x_v.at[mine], lsem.at[len(local)])
     x_direct = copy(x_in, x_v.at[mine], x_slot, sibling)
 
@@ -327,6 +338,15 @@
     def theirs_at(k):
         return x_v.at[theirs, pl.ds(k * piece, piece)]
 
+    res_copies = [
+        copy(res_v.at[:, pl.ds(k * piece, piece)], mine_at(k), x_prev_slots[k], at(pass_to, p)) for k in range(4)
+    ]
+
+    def pass_residual():
+        for k in range(4):
+            recv(res_v.at[:, pl.ds(k * piece, piece)], res_slots[k])
+            res_copies[k].start()
+
     pl.when(goes_early)(lambda: go(ph + RING))
     pl.when(does_far & (ph >= RING + 2))(help_far)
     pl.when(early_help)(help_halo)
@@ -358,6 +378,7 @@
         x_direct.wait_send()
         recv(x_v.at[theirs], x_slot)
 
+    pl.when(passes)(pass_residual)
     bl_slots = [next(slots) for _ in range(4)]
     bl_relay_slots = [next(slots) for _ in range(4)]
     bl_relays = [copy(bl_v.at[4 * j + h], bl_v.at[4 * j + h], bl_relay_slots[h], sibling) for h in range(4)]
@@ -553,10 +574,12 @@
         out_ref[:, n:n + step] = (x_v[mine, n:n + step].astype(jnp.float32) + update).astype(jnp.bfloat16)
     pl.when(ph + 1 < phases)(blended_last.wait_send)
     for k in range(4):
-        send(out_ref.at[:, pl.ds(k * piece, piece)], mine_at(k), x_prev_slots[k], ph_next2, res_out)
+        part = out_ref.at[:, pl.ds(k * piece, piece)]
+        send(part, mine_at(k), x_prev_slots[k], ph_next2, res_direct)
+        send(part, res_v.at[:, pl.ds(k * piece, piece)], res_slots[k], at(res_via, p), res_even)
 
     pl.when(late_help)(help_halo)
-    for made, when in pending + rel_copies + far_copies + [(via_mid, turn_out), (via_end, ph == 2)]:
+    for made, when in pending + rel_copies + far_copies + [(via_mid, turn_out), (via_end, ph == 2)] + [(made, passes) for made in res_copies]:
         if when is None:
             made.wait_send()
         else:
@@ -599,6 +622,7 @@
                 pltpu.VMEM((4, 2 * BLK, HEAD), jnp.bfloat16),
                 pltpu.VMEM((4, BLK, HEAD), jnp.bfloat16),
                 pltpu.VMEM((HEAD, width), jnp.bfloat16),
+                pltpu.VMEM((BLK, width), jnp.bfloat16),
                 pltpu.VMEM((2 * BLK, HEAD), jnp.float32),
                 pltpu.VMEM((4, 2 * BLK, HEAD), jnp.float32),
                 pltpu.VMEM((4, 2 * BLK, HEAD), jnp.float32),

time: 213 us -> 212 us (level)
  no operation moved by 1% of the time
where the time goes in v7:
time: 212 us; the launch traced here: 210 us
  Pallas kernels  208 us (98%)
    pallas_call x1, Pallas kernels, local(): pl.pallas_call(functools.partial(kernel, phases, chips), out_shape=jax.Sh...  208 us

profile of v7, /device:TPU:63, one launch (start us, length us, event | category | flops | bytes accessed | tf_op | source)
XLA Modules:
  0.0 209.7 jit_solution(9778584790267927537)
XLA Ops:
  0.0 207.8 %shard_map.55 = bf16[128,2048]{1,0:T(8,128)(2,1)} custom-call(bf16[128,2048]{1,0:T(8,128)(2,1)} %bitcast.8, s32[1,128]{1,0:T(1,128)} %seg_in.1, bf16[2048,1024]{1,0:T(8,128)(2,1)} %bitcast.5, bf16[64,2048]{1,0:T(8,128)(2,1)} %bitcast.9, bf16[8,128,2048]{2,1,0:T(8,128)(2,1)} %bitcast.6), custom_call_target="tpu_custom_call" | custom-call | tf_op jit(solution)/shard_map/pallas_call | solution.py:603
  207.8 1.9 copy.7

commit v8 on v7

--- a/solution.py
+++ b/solution.py
@@ -572,12 +572,13 @@
         update = jnp.dot(own, first, preferred_element_type=jnp.float32)
         update = update + jnp.dot(other, second, preferred_element_type=jnp.float32)
         out_ref[:, n:n + step] = (x_v[mine, n:n + step].astype(jnp.float32) + update).astype(jnp.bfloat16)
-    pl.when(ph + 1 < phases)(blended_last.wait_send)
+    pl.when((ph + 1 < phases) & (ph % 2 == 0))(blended_last.wait_send)
     for k in range(4):
         part = out_ref.at[:, pl.ds(k * piece, piece)]
         send(part, mine_at(k), x_prev_slots[k], ph_next2, res_direct)
         send(part, res_v.at[:, pl.ds(k * piece, piece)], res_slots[k], at(res_via, p), res_even)
 
+    pl.when((ph + 1 < phases) & (ph % 2 == 1))(blended_last.wait_send)
     pl.when(late_help)(help_halo)
     for made, when in pending + rel_copies + far_copies + [(via_mid, turn_out), (via_end, ph == 2)] + [(made, passes) for made in res_copies]:
         if when is None:

time: 212 us -> 212 us (level)
  no operation moved by 1% of the time
where the time goes in v8:
time: 212 us; the launch traced here: 209 us
  Pallas kernels  208 us (98%)
    pallas_call x1, Pallas kernels, local(): pl.pallas_call(functools.partial(kernel, phases, chips), out_shape=jax.Sh...  208 us

profile of v8, /device:TPU:63, one launch (start us, length us, event | category | flops | bytes accessed | tf_op | source)
XLA Modules:
  0.0 209.5 jit_solution(13494882876547142992)
XLA Ops:
  0.0 207.6 %shard_map.55 = bf16[128,2048]{1,0:T(8,128)(2,1)} custom-call(bf16[128,2048]{1,0:T(8,128)(2,1)} %bitcast.8, s32[1,128]{1,0:T(1,128)} %seg_in.1, bf16[2048,1024]{1,0:T(8,128)(2,1)} %bitcast.5, bf16[64,2048]{1,0:T(8,128)(2,1)} %bitcast.9, bf16[8,128,2048]{2,1,0:T(8,128)(2,1)} %bitcast.6), custom_call_target="tpu_custom_call" | custom-call | tf_op jit(solution)/shard_map/pallas_call | solution.py:604
  207.6 1.9 copy.7
